TPU v7x, 128 devices: a whole 4x4x4 slice. The times are simulated.
128 devices in a mesh: cells: 64 (over y, z, x), members: 2 (over core).
Axes of the slice: x: 4, y: 4, z: 4, core: 2. Of those that a mesh axis runs over, the one named last changes fastest.
Arguments:
- ensemble: float32 [64, 4, 65536], P('members', None, 'cells')
- speed: float32 [65536], P('cells'), may hold values from 0.1 to 0.85
- direction: int32 [65536], P('cells'), may hold values 0 or 1
- couple: float32 [4, 4], replicated, may hold values from -0.25 to 0.25
- obs_place: int32 [16384], P('cells'), may hold values from 0 to 1023
- obs_field: int32 [16384], P('cells'), may hold values from 0 to 3
- obs_value: float32 [16384], P('cells'), may hold values from -8 to 8
- obs_sigma: float32 [16384], P('cells'), may hold values from 0.5 to 5
- send_count: int32 [64, 64], P('cells'), may hold values from 0 to 32, as said below
Outputs:
- analysis: float32 [64, 4, 65536], P('members', None, 'cells')
- innovation: float32 [16384], P('cells')
Inputs may be any that keep to these rules, and one draw needn't show every extreme that they name: Each row of send_count sums to 256; no entry exceeds 32; in every row four blocks get exactly 32, and one block gets exactly 32 from every row.
All inputs are finite; a program needn't handle non-finite values. No bound on the sum of `direction` on one device may be relied on, other than what follows from the above.
Results may differ from a plain program's by a relative error of at most 0.0001.
Values sent between devices are 32-bit elements; how exact they have to be, the bound alone decides.
A program may use at most 64 MiB of HBM per device.

v0:
```python
import math

import jax
import jax.numpy as jnp
from jax import lax
from jax.sharding import PartitionSpec as P

STEPS = 4
OBS_DEV = 256
CAP = 32


DIFFUSION = 0.05


def padded_2(cells, sides, width):
    for axis, dim in sides:
        count = lax.axis_size(axis)
        ends = count - 1
        head = lax.slice_in_dim(cells, 0, width, axis=dim)
        tail = lax.slice_in_dim(cells, cells.shape[dim] - width, cells.shape[dim], axis=dim)
        cells = jnp.concatenate(
            [
                lax.ppermute(tail, axis, [(i, (i + 1) % count) for i in range(ends)]),
                cells,
                lax.ppermute(head, axis, [((i + 1) % count, i) for i in range(ends)]),
            ],
            axis=dim,
        )
    return cells


def factor_lower(matrix):
    order = matrix.shape[0]
    row_ids = jnp.arange(order, dtype=jnp.int32)

    def column_step(col, lower):
        column = lax.dynamic_slice_in_dim(matrix, col, 1, 1)[:, 0]
        done_row = lax.dynamic_slice_in_dim(lower, col, 1, 0)[0]
        reduced = column - jnp.dot(lower, done_row, precision=lax.Precision.HIGHEST)
        pivot = jnp.sqrt(lax.dynamic_slice_in_dim(reduced, col, 1, 0)[0])
        values = jnp.where(row_ids >= col, reduced / pivot, 0.0)
        return lax.dynamic_update_slice_in_dim(lower, values[:, None], col, 1)

    return lax.fori_loop(0, order, column_step, jnp.zeros_like(matrix))


def invert_lower(lower):
    order = lower.shape[0]
    identity = jnp.eye(order, dtype=jnp.float32)
    diagonal_values = jnp.diagonal(lower)
    nilpotent = identity - lower / diagonal_values[:, None]
    result = identity + nilpotent
    power = nilpotent
    for level in range(max(order - 1, 1).bit_length() - 1):
        power = jnp.dot(power, power, precision=lax.Precision.HIGHEST)
        result = jnp.dot(result, identity + power, precision=lax.Precision.HIGHEST)
    return result / diagonal_values[None, :]


def mixing_matrix(upper_factor, carried, members):
    upper_inverse = invert_lower(upper_factor.T).T
    mean_weights = jnp.dot(upper_inverse, carried, precision=lax.Precision.HIGHEST)
    identity = jnp.eye(members, dtype=jnp.float32)
    spread = math.sqrt(members - 1.0) * upper_inverse
    centering = identity - 1.0 / members
    shifted = jnp.dot(centering, mean_weights, precision=lax.Precision.HIGHEST)
    inner = jnp.dot(
        jnp.dot(centering, spread, precision=lax.Precision.HIGHEST),
        centering,
        precision=lax.Precision.HIGHEST,
    )
    return 1.0 / members + shifted[:, None] + inner


def couple_fields(couple, advanced):
    return advanced + jnp.einsum("fg,kgc->kfc", couple, advanced, precision=lax.Precision.HIGHEST)


def shards(
    ensemble, speed, direction, couple, obs_place, obs_field, obs_value, obs_sigma, send_count
):
    local_members, fields, cells_here = ensemble.shape
    owners = lax.axis_size("cells")
    members = local_members * lax.axis_size("members")
    flag_values = direction.astype(jnp.float32)
    toward_left = speed * flag_values
    toward_right = speed - toward_left
    states = ensemble
    for step_index in range(STEPS):
        padded = padded_2(states, (("cells", 2),), 1)
        left_cells = padded[:, :, :-2]
        right_cells = padded[:, :, 2:]
        advanced = (
            states
            + toward_left * left_cells
            + toward_right * right_cells
            - speed * states
            + DIFFUSION * (left_cells - 2.0 * states + right_cells)
        )
        states = couple_fields(couple, advanced)
    counts_row = send_count[0]
    owner_ends = jnp.cumsum(counts_row)
    starts = owner_ends - counts_row
    slot_ids = jnp.arange(OBS_DEV, dtype=jnp.int32)
    owner_of = jnp.sum((owner_ends[None, :] <= slot_ids[:, None]).astype(jnp.int32), axis=1)
    owner_match = owner_of[:, None] == jnp.arange(owners, dtype=jnp.int32)[None, :]
    start_of = jnp.sum(jnp.where(owner_match, starts[None, :], 0), axis=1)
    position = owner_of * CAP + slot_ids - start_of
    slot_grid = jnp.arange(CAP, dtype=jnp.int32)
    source_slot = jnp.minimum(starts[:, None] + slot_grid[None, :], OBS_DEV - 1)
    live_slot = slot_grid[None, :] < counts_row[:, None]
    request = jnp.where(live_slot, obs_field[source_slot] * cells_here + obs_place[source_slot], 0)
    flat_states = states.reshape(local_members, fields * cells_here)
    asked_slots = lax.all_to_all(request, "cells", split_axis=0, concat_axis=0, tiled=True)
    found_values = jnp.take(flat_states, asked_slots.reshape(-1), axis=1)
    found_values = found_values.reshape(local_members, asked_slots.shape[0], asked_slots.shape[1])
    returned = lax.all_to_all(found_values, "cells", split_axis=1, concat_axis=1, tiled=True)
    local_values = jnp.take(returned.reshape(local_members, owners * CAP), position, axis=1)
    all_values = lax.all_gather(local_values, "members", axis=0, tiled=True)
    center = jnp.mean(all_values, axis=0)
    scaled_anomaly = (all_values - center) / obs_sigma
    innovation = (obs_value - center) / obs_sigma
    augmented = jnp.concatenate([scaled_anomaly, innovation[None, :]], axis=0)
    local_gram = jnp.dot(augmented, augmented.T, precision=lax.Precision.HIGHEST)
    summed_gram = lax.psum(local_gram, "cells")
    diagonal_add = jnp.concatenate(
        [jnp.full((members,), members - 1.0, jnp.float32), jnp.ones((1,), jnp.float32)]
    )
    factor = factor_lower(summed_gram + jnp.diag(diagonal_add)).T
    mixing = mixing_matrix(factor[:members, :members], factor[:members, members], members)
    member_index = lax.axis_index("members")
    own_rows = lax.dynamic_slice_in_dim(mixing, member_index * local_members, local_members, 0)
    analysis = lax.psum_scatter(
        jnp.einsum("kj,kfc->jfc", own_rows, states, precision=lax.Precision.HIGHEST),
        "members",
        scatter_dimension=0,
        tiled=True,
    )
    return (analysis, innovation)


def solution(mesh):
    return jax.shard_map(
        shards,
        mesh=mesh,
        in_specs=(
            P("members", None, "cells"),
            P("cells"),
            P("cells"),
            P(),
            P("cells"),
            P("cells"),
            P("cells"),
            P("cells"),
            P("cells", None),
        ),
        out_specs=(P("members", None, "cells"), P("cells")),
        check_vma=False,
    )
```

profile of v0, /device:TPU:1, one launch (start us, length us, event | category | flops | bytes accessed | tf_op | source)
XLA Modules:
  0.0 626.4 jit_solution(9575588575575584767)
XLA Ops:
  8.2 3.9 collective-permute-start
  15.2 13.2 %gather_fusion = s32[2048]{0:T(1024)S(1)} fusion(s32[256]{0:T(256)S(1)} %copy-done.1, s32[2048]{0:T(1024)S(1)} %broadcast_clamp_fusion.1), kind=kCustom, calls=%fused_computation | custom fusion | bytes 24576 | tf_op jit(solution)/shard_map/gather | solution.py:113
  28.5 13.2 %gather_fusion.1 = s32[2048]{0:T(1024)S(1)} fusion(s32[256]{0:T(256)S(1)} %copy-done.2, s32[2048]{0:T(1024)S(1)} %broadcast_clamp_fusion.1), kind=kCustom, calls=%fused_computation.1 | custom fusion | bytes 24576 | tf_op jit(solution)/shard_map/gather | solution.py:113
  42.5 12.0 %all-to-all-start = ((s32[64,1,32]{2,1,0:T(1,128)}), s32[64,1,32]{2,1,0:T(1,128)S(1)}, u32[]{:S(2)}, u32[]{:S(2)}) async-start(s32[64,1,32]{2,1,0:T(1,128)} %bitcast.3), calls=%async_computation | async-start | bytes 65536 | tf_op jit(solution)/shard_map/all_to_all | solution.py:115
  54.7 2.2 fusion.10
  57.0 2.9 collective-permute-start.2
  61.3 3.8 collective-permute-done.3
  65.1 2.2 fusion.9
  67.4 2.9 collective-permute-start.4
  71.6 3.7 collective-permute-done.5
  75.3 2.2 fusion.8
  77.6 4.6 collective-permute-start.6
  83.8 3.5 collective-permute-done.7
  87.3 2.2 fusion.7
  91.5 7.6 %gather_fusion.2 = f32[2048,32]{1,0:T(8,128)} fusion(f32[32,4096]{0,1:T(8,128)S(1)} %bitcast.118, s32[2048]{0:T(1024)S(1)} %broadcast_clamp_fusion), kind=kCustom, calls=%fused_computation.2 | custom fusion | bytes 532480 | tf_op jit(solution)/shard_map/jit(_take)/gather | solution.py:116
  99.1 1.6 fusion.126
  101.9 18.0 %all-to-all-start.1 = ((f32[64,1,1024]{2,1,0:T(1,128)}), f32[64,1,1024]{2,1,0:T(1,128)S(1)}, u32[]{:S(2)}, u32[]{:S(2)}) async-start(f32[64,1,1024]{2,1,0:T(1,128)} %reshape.299), calls=%async_computation.1 | async-start | bytes 524288 | tf_op jit(solution)/shard_map/all_to_all | solution.py:118
  120.0 9.4 %all-to-all-done.1 = f32[64,1,1024]{2,1,0:T(1,128)S(1)} async-done(((f32[64,1,1024]{2,1,0:T(1,128)}), f32[64,1,1024]{2,1,0:T(1,128)S(1)}, u32[]{:S(2)}, u32[]{:S(2)}) %all-to-all-start.1) | async-done | bytes 262176 | tf_op jit(solution)/shard_map/all_to_all | solution.py:118
  132.4 8.5 %all_gather.3 = f32[64,256]{1,0:T(8,128)S(1)} all-gather(f32[32,256]{1,0:T(8,128)S(1)} %copy.36), channel_id=1, replica_groups=mesh['cells'=64,'members'=2] {'members'}, dimensions={0}, use_global_device_ids=true | all-gather | bytes 98304 | tf_op jit(solution)/shard_map/all_gather | solution.py:120
  141.2 288.0 %psum.7 = f32[65,65]{1,0:T(8,128)S(1)} all-reduce(f32[65,65]{1,0:T(8,128)S(1)} %fusion.76), channel_id=1, replica_groups=mesh['cells'=64,'members'=2] {'cells'}, use_global_device_ids=true, to_apply=%region_4.5 | all-reduce | flops 4225 | bytes 33800 | tf_op jit(solution)/shard_map/psum | solution.py:126
  429.4 120.6 %while.14 = (s32[]{:T(128)}, f32[65,65]{1,0:T(8,128)S(1)}, f32[65,65]{0,1:T(8,128)S(1)}, s32[]{:T(128)}, s32[]{:T(128)}) while((s32[]{:T(128)}, f32[65,65]{1,0:T(8,128)S(1)}, f32[65,65]{0,1:T(8,128)S(1)}, s32[]{:T(128)}, s32[]{:T(128)}) %tuple.49), condition=%wide.region_6.7_spmd.clone, body=%wide.region_5.6_spmd.clone.sunk | while | flops 50962 | bytes 40825 | solution.py:45
  553.6 3.5 fusion.89
  557.1 60.3 %reduce-scatter.2.cloned.1.call-done = f32[32,4,1024]{2,0,1:T(8,128)} async-done(((f32[64,4,1024]{2,0,1:T(8,128)}), f32[32,4,1024]{2,0,1:T(8,128)}) %reduce-scatter.2.cloned.1.call-update) | async-done | bytes 524304 | tf_op jit(solution)/shard_map/reduce_scatter | solution.py:134
  617.4 2.2 copy.39
  (420 shorter events, 93.1 us)
Async XLA Ops:
  7.2 47.5 %copy-start = (f32[4,4]{1,0:T(4,128)S(1)}, f32[4,4]{1,0:T(4,128)}, u32[]{:S(2)}) copy-start(f32[4,4]{1,0:T(4,128)} %param.14) | copy-start | bytes 196
  7.2 8.0 %copy-start.1 = (s32[256]{0:T(256)S(1)}, s32[256]{0:T(256)}, u32[]{:S(2)}) copy-start(s32[256]{0:T(256)} %param.16) | copy-start | bytes 3076
  8.2 46.5 %collective-permute-start = (f32[32,4,1]{2,1,0:T(4,128)S(1)}, f32[32,4,1]{2,1,0:T(4,128)S(1)}, u32[]{:S(2)}, u32[]{:S(2)}) collective-permute-start(f32[32,4,1]{2,1,0:T(4,128)S(1)} %get-tuple-element.122), channel_id=1, source_target_pairs={{0,2},{2,4},{4,6},{6,8},{8,10},{10,12},{12,14},{14,16},{16,18},{18... | collective-permute-start | bytes 1544 | tf_op jit(solution)/shard_map/ppermute | solution.py:24
  12.1 42.5 %collective-permute-start.1 = (f32[32,4,1]{2,1,0:T(4,128)S(1)}, f32[32,4,1]{2,1,0:T(4,128)S(1)}, u32[]{:S(2)}, u32[]{:S(2)}) collective-permute-start(f32[32,4,1]{2,1,0:T(4,128)S(1)} %get-tuple-element.123), channel_id=1, source_target_pairs={{2,0},{4,2},{6,4},{8,6},{10,8},{12,10},{14,12},{16,14},{18,16},{20... | collective-permute-start | bytes 1544 | tf_op jit(solution)/shard_map/ppermute | solution.py:26
  15.2 13.2 %copy-start.2 = (s32[256]{0:T(256)S(1)}, s32[256]{0:T(256)}, u32[]{:S(2)}) copy-start(s32[256]{0:T(256)} %param.15) | copy-start | bytes 3076
  28.4 13.3 %copy-start.8 = (s32[1,64]{1,0:T(1,128)S(1)}, s32[1,64]{1,0:T(1,128)}, u32[]{:S(2)}) copy-start(s32[1,64]{1,0:T(1,128)} %param.19) | copy-start | bytes 772
  28.4 26.1 %copy-start.6 = (s32[1024]{0:T(1024)S(1)}, s32[1024]{0:T(1024)}, u32[]{:S(2)}) copy-start(s32[1024]{0:T(1024)} %param.13) | copy-start | bytes 12292
  28.5 26.1 %copy-start.7 = (f32[1024]{0:T(1024)S(1)}, f32[1024]{0:T(1024)}, u32[]{:S(2)}) copy-start(f32[1024]{0:T(1024)} %param.12) | copy-start | bytes 12292
  28.5 26.2 %copy-start.3 = (f32[32,4,1024]{2,1,0:T(4,128)S(1)}, f32[32,4,1024]{2,1,0:T(4,128)}, u32[]{:S(2)}) copy-start(f32[32,4,1024]{2,1,0:T(4,128)} %param.11) | copy-start | bytes 1572868
  42.5 47.7 %all-to-all-start = ((s32[64,1,32]{2,1,0:T(1,128)}), s32[64,1,32]{2,1,0:T(1,128)S(1)}, u32[]{:S(2)}, u32[]{:S(2)}) async-start(s32[64,1,32]{2,1,0:T(1,128)} %bitcast.3), calls=%async_computation | async-start | bytes 65536 | tf_op jit(solution)/shard_map/all_to_all | solution.py:115
  57.0 4.3 collective-permute-start.2
  59.9 5.2 collective-permute-start.3
  67.4 4.2 collective-permute-start.4
  70.3 5.0 collective-permute-start.5
  77.6 6.1 collective-permute-start.6
  82.3 5.0 collective-permute-start.7
  100.7 40.2 %copy-start.4 = (f32[256]{0:T(256)S(1)}, f32[256]{0:T(256)}, u32[]{:S(2)}) copy-start(f32[256]{0:T(256)} %param.18) | copy-start | bytes 3076
  100.7 40.2 %copy-start.9 = (f32[256]{0:T(256)S(1)}, f32[256]{0:T(256)}, u32[]{:S(2)}) copy-start(f32[256]{0:T(256)} %param.17) | copy-start | bytes 3076
  101.9 327.3 %copy-start.10 = (f32[65]{0:T(128)S(1)}, f32[65]{0:T(128)}, u32[]{:S(2)}) copy-start(f32[65]{0:T(128)} %constant.99.clone.1) | copy-start | bytes 784
  101.9 27.5 %all-to-all-start.1 = ((f32[64,1,1024]{2,1,0:T(1,128)}), f32[64,1,1024]{2,1,0:T(1,128)S(1)}, u32[]{:S(2)}, u32[]{:S(2)}) async-start(f32[64,1,1024]{2,1,0:T(1,128)} %reshape.299), calls=%async_computation.1 | async-start | bytes 524288 | tf_op jit(solution)/shard_map/all_to_all | solution.py:118
  119.9 497.5 %reduce-scatter.2.cloned.1.call-start = ((), (), s32[]{:S(2)}) async-start(), calls=%async_computation.3 | async-start | bytes 1572864 | tf_op jit(solution)/shard_map/reduce_scatter | solution.py:134
  140.9 416.1 %copy-start.5 = (f32[256]{0:T(256)}, f32[256]{0:T(256)S(1)}, u32[]{:S(2)}) copy-start(f32[256]{0:T(256)S(1)} %get-tuple-element.127) | copy-start | bytes 3076
Sparse Core Ops, SparseCore 0:
  557.2 60.1 reduce-scatter.1
where the time goes:
time: 632 us; the launch traced here: 626 us
  blocking collectives  297 us (47%)
  local copies, waits for them, and re-layouts  107 us (17%)
  waiting for transfers between devices  80.7 us (13%)
  starting transfers between devices  49.8 us (8%)
  loops' own time  47.1 us (7%)
  matrix products  24.6 us (4%)
  between operations  14.6 us (2%)
    psum x1, blocking collectives, shards(): summed_gram = lax.psum(local_gram, 'cells')  288 us
    reduce_scatter x1, waiting for transfers between devices, shards(): lax.psum_scatter(jnp.einsum('kj,kfc->jfc', own_rows, states, precision=la...  60.3 us
    another operation x1, loops' own time, factor_lower(): return lax.fori_loop(0, order, column_step, jnp.zeros_like(matrix))  47.1 us
    dynamic_slice x65, local copies, waits for them, and re-layouts, column_step(): pivot = jnp.sqrt(lax.dynamic_slice_in_dim(reduced, col, 1, 0)[0])  40.3 us
    all_to_all x1, starting transfers between devices, shards(): lax.all_to_all(found_values, 'cells', split_axis=1, concat_axis=1, tiled=...  18 us
    dynamic_update_slice x65, local copies, waits for them, and re-layouts, column_step(): return lax.dynamic_update_slice_in_dim(lower, values[:, None], col, 1)  16.2 us
    ppermute x4, starting transfers between devices, padded_2(): lax.ppermute(tail, axis, [(i, (i + 1) % count) for i in range(ends)])  14.4 us
    gather x1, local copies, waits for them, and re-layouts, shards(): obs_field[source_slot] * cells_here + obs_place[source_slot]  13.2 us
  transfers between devices with their start and end apart: 11, of which 5 were waited for; matrix products, arithmetic and copies ran while one was open for 6% of the time, Pallas kernels for 0%

commit v1 on v0

v1 whole, which is shorter than its diff:
```python
import math

import jax
import jax.numpy as jnp
from jax import lax
from jax.experimental import pallas as pl
from jax.experimental.pallas import tpu as pltpu
from jax.sharding import PartitionSpec as P

STEPS = 4
DIFFUSION = 0.05
F = 4
K = 64
KL = 32
CELLS = 1024
HALF = 16
F32 = jnp.float32
I32 = jnp.int32
HIGHEST = lax.Precision.HIGHEST


def lanes_of(table, index):
    return jnp.take_along_axis(table, index, axis=1, mode="promise_in_bounds")


def kernel(
    ens, speed, direction, couple, place, field, value, sigma, counts,
    out, innov_out,
    states, split, coef, halo_out, halo_in, edge,
    m0, m1, m2, m3, slots, starts_s, counts_s, picked, innov_s,
    n0, n1, n2, n3, part, gy, gz, gx, gc, mix, send, recv, local,
):
    cells = lax.axis_index("cells")
    core = lax.axis_index("members")
    x = cells % 4
    z = (cells // 4) % 4
    y = cells // 16
    left_id = (cells + 63) % 64
    right_id = (cells + 1) % 64
    axes = {"x": (x, 1), "z": (z, 4), "y": (y, 16)}

    def peer(axis, step):
        mine, stride = axes[axis]
        other = (mine + step) % 4
        return other, {"cells": cells + (other - mine) * stride, "members": core}

    barrier = pltpu.get_barrier_semaphore()
    for axis in ("x", "z", "y"):
        for step in (1, 2, 3):
            pl.semaphore_signal(barrier, inc=1, device_id=peer(axis, step)[1])
    pl.semaphore_signal(barrier, inc=1, device_id={"cells": cells, "members": 1 - core})
    pl.semaphore_signal(barrier, inc=1, device_id={"cells": left_id, "members": core})
    pl.semaphore_signal(barrier, inc=1, device_id={"cells": right_id, "members": core})

    used = [0, 0]
    sent = []

    def copy_to(src, dst, device):
        at = used[0]
        used[0] += 1
        made = pltpu.make_async_remote_copy(
            src_ref=src, dst_ref=dst, send_sem=send.at[at], recv_sem=recv.at[at], device_id=device
        )
        made.start()
        sent.append(made)
        return made

    def copy_here(src, dst):
        at = used[1]
        used[1] += 1
        made = pltpu.make_async_copy(src, dst, local.at[at])
        made.start()
        return made

    def arrive(copies):
        for made in copies[:-1]:
            made.wait_recv()
        copies[-1].wait()

    lane = lax.broadcasted_iota(I32, (8, 128), 1)
    sub = lax.broadcasted_iota(I32, (8, 128), 0)
    lane64 = lax.broadcasted_iota(I32, (8, 64), 1)
    sub64 = lax.broadcasted_iota(I32, (8, 64), 0)

    flat = (field[...] * CELLS + place[...]).astype(F32)
    inverse = 1.0 / sigma[...]
    tables = []
    for quantity in (flat, value[...], inverse):
        tables.append([
            jnp.broadcast_to(quantity[:, h * 128 : (h + 1) * 128], (8, 128)) for h in (0, 1)
        ])
    count_row = jnp.broadcast_to(counts[...], (8, 64))

    def start_and_count(owner):
        begin = jnp.sum(jnp.where(lane64 < owner, count_row, 0), axis=1, keepdims=True)
        number = jnp.sum(jnp.where(lane64 == owner, count_row, 0), axis=1, keepdims=True)
        return begin, number

    slot = lane % 16
    which = (lane // 16) % 4
    upper = lane >= 64
    for g in range(4):
        row = sub64 + 8 * g
        base = (row // 2) % 4 * 4 + row // 8 + (row % 2) * 32
        b0, c0 = start_and_count(base)
        b1, c1 = start_and_count(base + 16)
        begin = jnp.where(upper, b1, b0)
        number = jnp.where(upper, c1, c0)
        rank = slot + HALF * core
        position = begin + rank
        low = position & 127
        second = position >= 128
        found = jnp.zeros((8, 128), F32)
        for q in range(3):
            got = jnp.where(second, lanes_of(tables[q][1], low), lanes_of(tables[q][0], low))
            found = jnp.where(which == q, got, found)
        found = jnp.where(rank < number, found, 0.0)
        m0[g] = found.reshape(4, 2, 1, 128)
    for g in range(8):
        row = sub64 + 8 * g
        begin, number = start_and_count(row % 4 * 16 + (row // 4) % 4 * 4 + row // 16)
        starts_s[8 * g : 8 * g + 8, :] = jnp.broadcast_to(begin, (8, 128))
        counts_s[8 * g : 8 * g + 8, :] = jnp.broadcast_to(number, (8, 128))

    toward_left = speed[...] * direction[...].astype(F32)
    for side, first in ((0, 896), (1, 0)):
        turned = jnp.transpose(ens[:, first : first + 128])
        halo_out[side, 0:8, :] = turned[120:128, :] if side == 0 else turned[0:8, :]
        halo_out[side, 8:9, :] = speed[:, first : first + 128]
        halo_out[side, 9:10, :] = toward_left[:, first : first + 128]
        halo_out[side, 10:16, :] = jnp.zeros((6, 128), F32)

    pl.semaphore_wait(barrier, 12)

    halo = [
        copy_to(halo_out.at[0], halo_in.at[0], {"cells": right_id, "members": core}),
        copy_to(halo_out.at[1], halo_in.at[1], {"cells": left_id, "members": core}),
    ]

    def exchange(axis, src_of, dst):
        made = [copy_to(src_of(peer(axis, s)[0]), dst, peer(axis, s)[1]) for s in (1, 2, 3)]
        return made + [copy_here(src_of(axes[axis][0]), dst)]

    going = exchange("x", lambda o: m0.at[o], m1.at[x])

    speed_row = speed[...]
    coef[0, :, 0:CELLS] = jnp.broadcast_to(1.0 - 2.0 * DIFFUSION - speed_row, (8, CELLS))
    coef[1, :, 0:CELLS] = jnp.broadcast_to(toward_left + DIFFUSION, (8, CELLS))
    coef[2, :, 0:CELLS] = jnp.broadcast_to(speed_row - toward_left + DIFFUSION, (8, CELLS))

    arrive(going)
    going = exchange("z", lambda o: m1.at[:, o], m2.at[z])

    for made in halo:
        made.wait_recv()
    has_left = jnp.where(cells > 0, 1.0, 0.0).astype(F32)
    has_right = jnp.where(cells < 63, 1.0, 0.0).astype(F32)
    present = jnp.where(lane < 64, has_right, has_left)
    edge[0:8, :] = halo_in[1, 0:8, :] * has_right
    edge[8:120, :] = jnp.zeros((112, 128), F32)
    edge[120:128, :] = halo_in[0, 0:8, :] * has_left
    edge[...] = jnp.transpose(edge[...])
    edge_speed = jnp.where(lane < 64, halo_in[1, 8:9, :], halo_in[0, 8:9, :])
    edge_left = jnp.where(lane < 64, halo_in[1, 9:10, :], halo_in[0, 9:10, :])
    coef[0, :, CELLS:] = present * (1.0 - 2.0 * DIFFUSION - edge_speed)
    coef[1, :, CELLS:] = present * (edge_left + DIFFUSION)
    coef[2, :, CELLS:] = present * (edge_speed - edge_left + DIFFUSION)

    def advance(group, carry):
        rows = pl.multiple_of(group * 8, 8)
        now = [
            jnp.concatenate([ens[pl.ds(f * KL + rows, 8), :], edge[pl.ds(f * KL + rows, 8), :]], axis=1)
            for f in range(F)
        ]
        for _ in range(STEPS):
            moved = [
                coef[0] * u
                + coef[1] * pltpu.roll(u, 1, 1)
                + coef[2] * pltpu.roll(u, CELLS + 127, 1)
                for u in now
            ]
            now = [
                moved[f] + sum(couple[f, g] * moved[g] for g in range(F)) for f in range(F)
            ]
        for f in range(F):
            states[f, pl.ds(pl.multiple_of(core * KL + rows, 8), 8), :] = now[f][:, 0:CELLS]
        return carry

    lax.fori_loop(0, 4, advance, 0)

    mine = states.at[:, pl.ds(pl.multiple_of(core * KL, KL), KL), :]
    swap = copy_to(mine, mine, {"cells": cells, "members": 1 - core})

    arrive(going)
    going = exchange("y", lambda o: m2.at[:, :, o // 2], m3.at[y])
    arrive(going)

    off = (y % 2) * 64
    for r in range(8):
        rows = m3[r // 2, 2 * (r % 2) : 2 * (r % 2) + 2].reshape(8, 128)
        for q in range(3):
            got = lanes_of(rows, off + 16 * q + slot)
            got = jnp.where(lane // 16 == sub, got, 0.0)
            slots[q, r : r + 1, :] = jnp.sum(got, axis=0, keepdims=True)

    swap.wait_recv()

    def pick(r, carry):
        index = jnp.broadcast_to(slots[0, pl.ds(r, 1), :], (8, 128)).astype(I32)
        low = index & 127
        high = index // 128
        found = [jnp.zeros((8, 128), F32)] * 8
        for c in range(32):
            here = high == c
            for g in range(8):
                tile = states[c // 8, 8 * g : 8 * g + 8, (c % 8) * 128 : (c % 8) * 128 + 128]
                found[g] = jnp.where(here, lanes_of(tile, low), found[g])
        total = found[0]
        for g in range(1, 8):
            total = total + found[g]
        center = jnp.sum(total, axis=0, keepdims=True) / K
        scale = slots[2, pl.ds(r, 1), :]
        at = pl.ds(pl.multiple_of(r * 128, 128), 128)
        for g in range(8):
            picked[8 * g : 8 * g + 8, at] = (found[g] - center) * scale
        row = (slots[1, pl.ds(r, 1), :] - center) * scale
        innov_s[:, at] = jnp.where(sub == 0, row, 0.0)
        n0[r] = row
        return carry

    lax.fori_loop(0, 8, pick, 0)

    contract = (((1,), (1,)), ((), ()))
    anomalies = picked[...]
    gram = lax.dot_general(anomalies, anomalies, contract, precision=HIGHEST, preferred_element_type=F32)
    cross = lax.dot_general(innov_s[...], anomalies, contract, precision=HIGHEST, preferred_element_type=F32)
    gy[y, 0:32, :] = jnp.concatenate([gram[0:32], gram[32:64]], axis=1)
    gy[y, 32:40, :] = jnp.concatenate([cross, jnp.zeros((8, 64), F32)], axis=1)

    def share(axis, ref):
        at = axes[axis][0]
        return [copy_to(ref.at[at], ref.at[at], peer(axis, s)[1]) for s in (1, 2, 3)]

    def collect(copies, ref):
        for made in copies:
            made.wait_recv()
        return (ref[0] + ref[1]) + (ref[2] + ref[3])

    adding = share("y", gy)
    back = exchange("y", lambda o: n0.at[pl.ds(2 * o, 2)], n1.at[y])

    for f in range(F):
        full = states[f]
        head = full.astype(jnp.bfloat16)
        split[f, 0:K, :] = head
        split[f, K : 2 * K, :] = (full - head.astype(F32)).astype(jnp.bfloat16)

    gz[z] = collect(adding, gy)
    adding = share("z", gz)
    arrive(back)
    back = exchange("z", lambda o: n1.at[:, o // 2], n2.at[z])

    gx[x] = collect(adding, gz)
    adding = share("x", gx)
    arrive(back)
    back = exchange("x", lambda o: n2, n3.at[x])

    gc[core] = collect(adding, gx)
    adding = copy_to(gc.at[core], gc.at[core], {"cells": cells, "members": 1 - core})

    arrive(back)
    shift = 64 * (z % 2) + 16 * x - HALF * core
    totals = [jnp.zeros((8, 128), F32)] * 2
    for g in range(8):
        rows = n3[g // 2, 2 * (g % 2) : 2 * (g % 2) + 2].reshape(8, 128)
        begin = starts_s[8 * g : 8 * g + 8, :]
        number = counts_s[8 * g : 8 * g + 8, :]
        for t in range(2):
            rank = lane + 128 * t - begin
            inside = rank - HALF * core
            good = (inside >= 0) & (inside < HALF) & (rank < number)
            got = lanes_of(rows, (rank + shift) & 127)
            totals[t] = totals[t] + jnp.where(good, got, 0.0)
    for t in range(2):
        part[core, t] = jnp.sum(totals[t], axis=0, keepdims=True)
    joined = copy_to(part.at[core], part.at[core], {"cells": cells, "members": 1 - core})

    adding.wait_recv()
    total = gc[0] + gc[1]

    a = []
    for h in range(8):
        packed = total[8 * (h % 4) : 8 * (h % 4) + 8]
        packed = packed if h < 4 else pltpu.roll(packed, 64, 1)
        packed = jnp.where(lane == sub + 8 * h, packed + (K - 1.0), packed)
        a.append(jnp.where(lane < K, packed, 0.0))
    pivots = [jnp.ones((8, 128), F32)] * 8
    for k in range(K):
        g, i = k // 8, k % 8
        at_k = lane == k
        row = jnp.broadcast_to(a[g][i : i + 1, :], (8, 128))
        pivot = jnp.broadcast_to(row[:, k : k + 1], (8, 128))
        over = 1.0 / pivot
        unit = jnp.where(at_k, 1.0, row)
        pivots[g] = jnp.where(sub == i, pivot, pivots[g])
        for h in range(g, 8):
            factor = jnp.broadcast_to(a[h][:, k : k + 1], (8, 128)) * over
            if h == g:
                factor = jnp.where(sub > i, factor, 0.0)
                kept = jnp.where(at_k & (sub > i), 0.0, a[h])
            else:
                kept = jnp.where(at_k, 0.0, a[h])
            a[h] = kept - factor * unit
    inv = []
    for h in range(8):
        row_id = sub + 8 * h
        unit = jnp.where(lane < row_id, a[h], jnp.where(lane == row_id, 1.0, 0.0))
        inv.append(unit / jnp.sqrt(pivots[h]))
    cross_row = jnp.where(lane[0:1] < K, total[32:33, :], 0.0)
    columns = jnp.zeros((8, 128), F32)
    weights = jnp.zeros((8, 128), F32)
    means = []
    for h in range(8):
        columns = columns + inv[h]
        means.append(jnp.sum(inv[h], axis=1, keepdims=True) / K)
        carried = jnp.sum(inv[h] * cross_row, axis=1, keepdims=True)
        weights = weights + inv[h] * carried
    column_mean = jnp.sum(columns, axis=0, keepdims=True) / K
    weight_row = jnp.sum(weights, axis=0, keepdims=True)
    grand = jnp.sum(column_mean, axis=1, keepdims=True) / K
    shifted = weight_row - jnp.sum(weight_row, axis=1, keepdims=True) / K + 1.0 / K
    for h in range(8):
        inner = inv[h] - means[h] - column_mean + grand
        rows = shifted + math.sqrt(K - 1.0) * inner
        mix[8 * h : 8 * h + 8, :] = jnp.where(lane < K, rows, pltpu.roll(rows, 64, 1))

    own = mix[pl.ds(pl.multiple_of(core * KL, KL), KL), :]
    head = own.astype(jnp.bfloat16)
    tail = (own - head.astype(F32)).astype(jnp.bfloat16)
    both = jnp.concatenate([head, tail], axis=0)
    for f in range(F):
        product = jnp.dot(both, split[f], preferred_element_type=F32)
        out[f] = product[0:KL] + product[KL : 2 * KL]

    joined.wait_recv()
    for t in range(2):
        innov_out[t : t + 1, :] = part[0, t] + part[1, t]
    for made in sent:
        made.wait_send()


def shards(
    ensemble, speed, direction, couple, obs_place, obs_field, obs_value, obs_sigma, send_count
):
    vmem = pl.BlockSpec(memory_space=pltpu.VMEM)
    smem = pl.BlockSpec(memory_space=pltpu.SMEM)
    row = lambda a: a.reshape(1, -1)
    by_field = jnp.transpose(ensemble, (1, 0, 2)).reshape(F * KL, CELLS)
    analysis, innovation = pl.pallas_call(
        kernel,
        out_shape=(
            jax.ShapeDtypeStruct((F, KL, CELLS), F32),
            jax.ShapeDtypeStruct((2, 128), F32),
        ),
        in_specs=[vmem, vmem, vmem, smem, vmem, vmem, vmem, vmem, vmem],
        out_specs=(vmem, vmem),
        scratch_shapes=[
            pltpu.VMEM((F, K, CELLS), F32),
            pltpu.VMEM((F, 2 * K, CELLS), jnp.bfloat16),
            pltpu.VMEM((3, 8, CELLS + 128), F32),
            pltpu.VMEM((2, 16, 128), F32),
            pltpu.VMEM((2, 16, 128), F32),
            pltpu.VMEM((128, 128), F32),
            pltpu.VMEM((4, 4, 2, 1, 128), F32),
            pltpu.VMEM((4, 4, 2, 1, 128), F32),
            pltpu.VMEM((4, 4, 2, 1, 128), F32),
            pltpu.VMEM((4, 4, 4, 1, 128), F32),
            pltpu.VMEM((3, 8, 128), F32),
            pltpu.VMEM((64, 128), I32),
            pltpu.VMEM((64, 128), I32),
            pltpu.VMEM((K, CELLS), F32),
            pltpu.VMEM((8, CELLS), F32),
            pltpu.VMEM((8, 1, 128), F32),
            pltpu.VMEM((4, 2, 1, 128), F32),
            pltpu.VMEM((4, 4, 1, 128), F32),
            pltpu.VMEM((4, 4, 4, 1, 128), F32),
            pltpu.VMEM((2, 2, 1, 128), F32),
            pltpu.VMEM((4, 40, 128), F32),
            pltpu.VMEM((4, 40, 128), F32),
            pltpu.VMEM((4, 40, 128), F32),
            pltpu.VMEM((2, 40, 128), F32),
            pltpu.VMEM((K, 128), F32),
            pltpu.SemaphoreType.DMA((32,)),
            pltpu.SemaphoreType.DMA((32,)),
            pltpu.SemaphoreType.DMA((6,)),
        ],
        compiler_params=pltpu.CompilerParams(collective_id=0, has_side_effects=True),
    )(
        by_field, row(speed), row(direction), couple, row(obs_place), row(obs_field),
        row(obs_value), row(obs_sigma), send_count,
    )
    return jnp.transpose(analysis, (1, 0, 2)), innovation.reshape(256)


def solution(mesh):
    return jax.shard_map(
        shards,
        mesh=mesh,
        in_specs=(
            P("members", None, "cells"),
            P("cells"),
            P("cells"),
            P(),
            P("cells"),
            P("cells"),
            P("cells"),
            P("cells"),
            P("cells", None),
        ),
        out_specs=(P("members", None, "cells"), P("cells")),
        check_vma=False,
    )
```

time: 632 us -> 54.2 us (0.09)
  blocking collectives: 297 us -> 0 us
  local copies, waits for them, and re-layouts: 107 us -> 5.55 us
  waiting for transfers between devices: 80.7 us -> 0 us
  starting transfers between devices: 49.8 us -> 0 us
  Pallas kernels: 0 us -> 47.8 us
  loops' own time: 47.1 us -> 0 us
  matrix products: 24.6 us -> 0 us
  between operations: 14.6 us -> 0.64 us
    psum x1 -> x0, blocking collectives: 288 us -> none  [shards(): summed_gram = lax.psum(local_gram, 'cells')]
    reduce_scatter x1 -> x0, waiting for transfers between devices: 60.3 us -> none  [shards(): lax.psum_scatter(jnp.einsum('kj,kfc->jfc', own_rows, states, precision=la...]
    pallas_call x0 -> x1, Pallas kernels: none -> 47.8 us  [shards(): pl.pallas_call(kernel, out_shape=(jax.ShapeDtypeStruct((F, KL, CELLS), F3...]
    another operation x1 -> x0, loops' own time: 47.1 us -> none  [factor_lower(): return lax.fori_loop(0, order, column_step, jnp.zeros_like(matrix))]
    dynamic_slice x66 -> x0, local copies, waits for them, and re-layouts: 40.3 us -> none  [the longest x65 40.3 us: column_step(): pivot = jnp.sqrt(lax.dynamic_slice_in_dim(reduced, col, 1, 0)[0])]
    gather x5 -> x0, local copies, waits for them, and re-layouts: 35.6 us -> none  [the longest x1 13.2 us: shards(): obs_field[source_slot] * cells_here + obs_place[source_slot]]
    all_to_all x2 -> x0, starting transfers between devices: 30 us -> none  [the longest x1 18 us: shards(): lax.all_to_all(found_values, 'cells', split_axis=1, concat_axis=1, tiled=...]
    dot_general x85 -> x0, matrix products: 24.6 us -> none  [the longest x65 9.58 us: column_step(): reduced = column - jnp.dot(lower, done_row, precision=lax.Precision.HIGHEST)]
  transfers between devices with their start and end apart: 11 -> 0, of which waited for: 5 -> 0; matrix products, arithmetic and copies ran while one was open for 6% -> 0% of each run, Pallas kernels for 0% -> 0%
where the time goes in v1:
time: 54.2 us; the launch traced here: 53.9 us
  Pallas kernels  47.8 us (88%)
  local copies, waits for them, and re-layouts  5.55 us (10%)
  between operations  0.64 us (1%)
    pallas_call x1, Pallas kernels, shards(): pl.pallas_call(kernel, out_shape=(jax.ShapeDtypeStruct((F, KL, CELLS), F3...  47.8 us
    unnamed x4, local copies, waits for them, and re-layouts  3.41 us
    transpose x1, local copies, waits for them, and re-layouts, shards(): by_field = jnp.transpose(ensemble, (1, 0, 2)).reshape(F * KL, CELLS)  2.14 us

profile of v1, /device:TPU:1, one launch (start us, length us, event | category | flops | bytes accessed | tf_op | source)
XLA Modules:
  0.0 53.9 jit_solution(7308522853394482543)
XLA Ops:
  0.6 2.1 %copy.11 = f32[4,32,1024]{2,1,0:T(8,128)} copy(f32[4,32,1024]{2,0,1:T(4,128)} %bitcast.11) | data formatting | bytes 1048576 | tf_op jit(solution)/shard_map/transpose | solution.py:358
  2.8 47.8 %shard_map.104 = (f32[4,32,1024]{2,1,0:T(8,128)}, f32[2,128]{1,0:T(2,128)}) custom-call(f32[128,1024]{1,0:T(8,128)} %bitcast.10, f32[1,1024]{1,0:T(1,128)} %bitcast.13, s32[1,1024]{1,0:T(1,128)} %bitcast.14, f32[4,4]{1,0:T(4,128)} %couple.1, s32[1,256]{1,0:T(1,128)} %bitcast.15, s32[1,256]{1,0:T(1,128)} %bitcast.16, f32[1,256]{1,0:T(1,128)} %bitcast.17, ...), custom_call_target="tpu_custom_call" | custom-call | tf_op jit(solution)/shard_map/pallas_call | solution.py:359
  50.5 2.2 %copy.12 = f32[32,4,1024]{2,1,0:T(4,128)} copy(f32[32,4,1024]{2,0,1:T(8,128)} %bitcast.12) | data formatting | bytes 1048576
  52.7 0.0 copy-start
  52.7 0.7 %copy-done = f32[2,128]{1,0:T(2,128)S(1)} copy-done((f32[2,128]{1,0:T(2,128)S(1)}, f32[2,128]{1,0:T(2,128)}, u32[]{:S(2)}) %copy-start) | copy-done | bytes 1048
  53.4 0.6 %copy.14 = f32[256]{0:T(256)} copy(f32[256]{0:T(256)S(1)} %bitcast.19) | data formatting | bytes 2048
Async XLA Ops:
  52.7 0.7 %copy-start = (f32[2,128]{1,0:T(2,128)S(1)}, f32[2,128]{1,0:T(2,128)}, u32[]{:S(2)}) copy-start(f32[2,128]{1,0:T(2,128)} %get-tuple-element.5) | copy-start | bytes 3076

commit v2 on v1

--- a/solution.py
+++ b/solution.py
@@ -24,11 +24,12 @@
 
 
 def kernel(
-    ens, speed, direction, couple, place, field, value, sigma, counts,
-    out, innov_out,
+    ens_hbm, speed_hbm, direction_hbm, couple_hbm, place_hbm, field_hbm, value_hbm, sigma_hbm,
+    counts_hbm, out_hbm, innov_out,
+    ens, out, speed, direction, couple, place, field, value, sigma, counts,
     states, split, coef, halo_out, halo_in, edge,
-    m0, m1, m2, m3, slots, starts_s, counts_s, picked, innov_s,
-    n0, n1, n2, n3, part, gy, gz, gx, gc, mix, send, recv, local,
+    m0, m1, m2, m3, starts_s, counts_s, picked, innov_s,
+    n0, n1, n2, n3, part, gy, gz, gx, gc, mix, send, recv, local, bulk,
 ):
     cells = lax.axis_index("cells")
     core = lax.axis_index("members")
@@ -52,6 +53,17 @@
     pl.semaphore_signal(barrier, inc=1, device_id={"cells": left_id, "members": core})
     pl.semaphore_signal(barrier, inc=1, device_id={"cells": right_id, "members": core})
 
+    small = (
+        (counts_hbm, counts), (place_hbm, place), (field_hbm, field), (value_hbm, value),
+        (sigma_hbm, sigma), (speed_hbm, speed), (direction_hbm, direction), (couple_hbm, couple),
+    )
+    early = [pltpu.make_async_copy(src, dst, bulk.at[F + i]) for i, (src, dst) in enumerate(small)]
+    loads = [
+        pltpu.make_async_copy(ens_hbm.at[:, f], ens.at[pl.ds(f * KL, KL)], bulk.at[f]) for f in range(F)
+    ]
+    for made in early + loads:
+        made.start()
+
     used = [0, 0]
     sent = []
 
@@ -82,6 +94,8 @@
     lane64 = lax.broadcasted_iota(I32, (8, 64), 1)
     sub64 = lax.broadcasted_iota(I32, (8, 64), 0)
 
+    for made in early:
+        made.wait()
     flat = (field[...] * CELLS + place[...]).astype(F32)
     inverse = 1.0 / sigma[...]
     tables = []
@@ -122,6 +136,8 @@
         starts_s[8 * g : 8 * g + 8, :] = jnp.broadcast_to(begin, (8, 128))
         counts_s[8 * g : 8 * g + 8, :] = jnp.broadcast_to(number, (8, 128))
 
+    for made in loads:
+        made.wait()
     toward_left = speed[...] * direction[...].astype(F32)
     for side, first in ((0, 896), (1, 0)):
         turned = jnp.transpose(ens[:, first : first + 128])
@@ -143,10 +159,44 @@
 
     going = exchange("x", lambda o: m0.at[o], m1.at[x])
 
+    gain = [[couple[f, g] + (1.0 if f == g else 0.0) for g in range(F)] for f in range(F)]
+    for _ in range(2):
+        gain = [
+            [sum(gain[f][e] * gain[e][g] for e in range(F)) for g in range(F)] for f in range(F)
+        ]
     speed_row = speed[...]
     coef[0, :, 0:CELLS] = jnp.broadcast_to(1.0 - 2.0 * DIFFUSION - speed_row, (8, CELLS))
     coef[1, :, 0:CELLS] = jnp.broadcast_to(toward_left + DIFFUSION, (8, CELLS))
     coef[2, :, 0:CELLS] = jnp.broadcast_to(speed_row - toward_left + DIFFUSION, (8, CELLS))
+
+    def transport(u, centre, from_left, from_right):
+        width = u.shape[1]
+        for _ in range(STEPS):
+            u = (
+                centre * u
+                + from_left * pltpu.roll(u, 1, 1)
+                + from_right * pltpu.roll(u, width - 1, 1)
+            )
+        return u
+
+    def coupled(moved):
+        return [sum(gain[f][g] * moved[g] for g in range(F)) for f in range(F)]
+
+    def interior(group, carry):
+        rows = pl.multiple_of(group * 8, 8)
+        into = pl.ds(pl.multiple_of(core * KL + rows, 8), 8)
+        moved = [
+            transport(
+                ens[pl.ds(f * KL + rows, 8), :],
+                coef[0, :, 0:CELLS], coef[1, :, 0:CELLS], coef[2, :, 0:CELLS],
+            )
+            for f in range(F)
+        ]
+        for f, made in enumerate(coupled(moved)):
+            states[f, into, :] = made
+        return carry
+
+    lax.fori_loop(0, 4, interior, 0)
 
     arrive(going)
     going = exchange("z", lambda o: m1.at[:, o], m2.at[z])
@@ -162,51 +212,71 @@
     edge[...] = jnp.transpose(edge[...])
     edge_speed = jnp.where(lane < 64, halo_in[1, 8:9, :], halo_in[0, 8:9, :])
     edge_left = jnp.where(lane < 64, halo_in[1, 9:10, :], halo_in[0, 9:10, :])
-    coef[0, :, CELLS:] = present * (1.0 - 2.0 * DIFFUSION - edge_speed)
-    coef[1, :, CELLS:] = present * (edge_left + DIFFUSION)
-    coef[2, :, CELLS:] = present * (edge_speed - edge_left + DIFFUSION)
-
-    def advance(group, carry):
+    around = (
+        present * (1.0 - 2.0 * DIFFUSION - edge_speed),
+        present * (edge_left + DIFFUSION),
+        present * (edge_speed - edge_left + DIFFUSION),
+    )
+    strip = [
+        jnp.concatenate([coef[i, :, CELLS - 128 :], around[i], coef[i, :, 0:128]], axis=1)
+        for i in range(3)
+    ]
+
+    def border(group, carry):
         rows = pl.multiple_of(group * 8, 8)
-        now = [
-            jnp.concatenate([ens[pl.ds(f * KL + rows, 8), :], edge[pl.ds(f * KL + rows, 8), :]], axis=1)
-            for f in range(F)
-        ]
-        for _ in range(STEPS):
-            moved = [
-                coef[0] * u
-                + coef[1] * pltpu.roll(u, 1, 1)
-                + coef[2] * pltpu.roll(u, CELLS + 127, 1)
-                for u in now
-            ]
-            now = [
-                moved[f] + sum(couple[f, g] * moved[g] for g in range(F)) for f in range(F)
-            ]
+        into = pl.ds(pl.multiple_of(core * KL + rows, 8), 8)
+        moved = []
         for f in range(F):
-            states[f, pl.ds(pl.multiple_of(core * KL + rows, 8), 8), :] = now[f][:, 0:CELLS]
+            at = pl.ds(f * KL + rows, 8)
+            u = jnp.concatenate([ens[at, CELLS - 128 :], edge[at, :], ens[at, 0:128]], axis=1)
+            moved.append(transport(u, *strip))
+        for f, made in enumerate(coupled(moved)):
+            before = states[f, into, CELLS - 128 :]
+            states[f, into, CELLS - 128 :] = jnp.where(lane >= 64, made[:, 0:128], before)
+            after = states[f, into, 0:128]
+            states[f, into, 0:128] = jnp.where(lane < 64, made[:, 256:384], after)
         return carry
 
-    lax.fori_loop(0, 4, advance, 0)
+    lax.fori_loop(0, 4, border, 0)
 
     mine = states.at[:, pl.ds(pl.multiple_of(core * KL, KL), KL), :]
     swap = copy_to(mine, mine, {"cells": cells, "members": 1 - core})
 
     arrive(going)
-    going = exchange("y", lambda o: m2.at[:, :, o // 2], m3.at[y])
-    arrive(going)
+    base = used[0]
+    used[0] += 4
+    own_rows = pltpu.make_async_copy(m2.at[:, :, y // 2], m3.at[y], recv.at[base])
+    own_rows.start()
+    for step in (1, 3, 2):
+        o, device = peer("y", step)
+        made = pltpu.make_async_remote_copy(
+            src_ref=m2.at[:, :, o // 2], dst_ref=m3.at[y],
+            send_sem=send.at[base + step], recv_sem=recv.at[base + step], device_id=device,
+        )
+        made.start()
+        sent.append(made)
+    swap.wait_recv()
 
     off = (y % 2) * 64
-    for r in range(8):
-        rows = m3[r // 2, 2 * (r % 2) : 2 * (r % 2) + 2].reshape(8, 128)
+
+    def pick(turn, carry):
+        t = turn // 2
+        step = t + t // 2 - 2 * (t // 3)
+        source = (y + 4 - step) % 4
+        pair = turn % 2
+        r = source * 2 + pair
+
+        @pl.when(pair == 0)
+        def _():
+            pltpu.make_async_copy(m3.at[source], m3.at[source], recv.at[base + step]).wait()
+
+        rows = m3[source, pl.ds(2 * pair, 2)].reshape(8, 128)
+        asked = []
         for q in range(3):
             got = lanes_of(rows, off + 16 * q + slot)
             got = jnp.where(lane // 16 == sub, got, 0.0)
-            slots[q, r : r + 1, :] = jnp.sum(got, axis=0, keepdims=True)
-
-    swap.wait_recv()
-
-    def pick(r, carry):
-        index = jnp.broadcast_to(slots[0, pl.ds(r, 1), :], (8, 128)).astype(I32)
+            asked.append(jnp.sum(got, axis=0, keepdims=True))
+        index = jnp.broadcast_to(asked[0], (8, 128)).astype(I32)
         low = index & 127
         high = index // 128
         found = [jnp.zeros((8, 128), F32)] * 8
@@ -219,11 +289,10 @@
         for g in range(1, 8):
             total = total + found[g]
         center = jnp.sum(total, axis=0, keepdims=True) / K
-        scale = slots[2, pl.ds(r, 1), :]
         at = pl.ds(pl.multiple_of(r * 128, 128), 128)
         for g in range(8):
-            picked[8 * g : 8 * g + 8, at] = (found[g] - center) * scale
-        row = (slots[1, pl.ds(r, 1), :] - center) * scale
+            picked[8 * g : 8 * g + 8, at] = (found[g] - center) * asked[2]
+        row = (asked[1] - center) * asked[2]
         innov_s[:, at] = jnp.where(sub == 0, row, 0.0)
         n0[r] = row
         return carry
@@ -294,28 +363,59 @@
         packed = packed if h < 4 else pltpu.roll(packed, 64, 1)
         packed = jnp.where(lane == sub + 8 * h, packed + (K - 1.0), packed)
         a.append(jnp.where(lane < K, packed, 0.0))
-    pivots = [jnp.ones((8, 128), F32)] * 8
-    for k in range(K):
-        g, i = k // 8, k % 8
-        at_k = lane == k
-        row = jnp.broadcast_to(a[g][i : i + 1, :], (8, 128))
-        pivot = jnp.broadcast_to(row[:, k : k + 1], (8, 128))
-        over = 1.0 / pivot
-        unit = jnp.where(at_k, 1.0, row)
-        pivots[g] = jnp.where(sub == i, pivot, pivots[g])
-        for h in range(g, 8):
-            factor = jnp.broadcast_to(a[h][:, k : k + 1], (8, 128)) * over
-            if h == g:
-                factor = jnp.where(sub > i, factor, 0.0)
-                kept = jnp.where(at_k & (sub > i), 0.0, a[h])
-            else:
-                kept = jnp.where(at_k, 0.0, a[h])
-            a[h] = kept - factor * unit
     inv = []
-    for h in range(8):
-        row_id = sub + 8 * h
-        unit = jnp.where(lane < row_id, a[h], jnp.where(lane == row_id, 1.0, 0.0))
-        inv.append(unit / jnp.sqrt(pivots[h]))
+    for g in range(8):
+        first = 8 * g
+        block = a[g]
+        inside = (lane >= first) & (lane < first + 8)
+
+        def column(rows, j):
+            return jnp.broadcast_to(rows[:, first + j : first + j + 1], (8, 128))
+
+        def spread_row(rows, i):
+            return jnp.broadcast_to(rows[i : i + 1, :], (8, 128))
+
+        columns = [column(block, j) for j in range(8)]
+        d = {(i, j): spread_row(columns[j], i) for j in range(8) for i in range(j, 8)}
+        over, low = [], {}
+        for k in range(8):
+            over.append(1.0 / d[k, k])
+            for i in range(k + 1, 8):
+                low[i, k] = d[i, k] * over[k]
+            for j in range(k + 1, 8):
+                for i in range(j, 8):
+                    d[i, j] = d[i, j] - low[i, k] * d[j, k]
+        m = {}
+        for i in range(8):
+            for j in range(i):
+                total_ij = low[i, j]
+                for e in range(j + 1, i):
+                    total_ij = total_ij + low[i, e] * m[e, j]
+                m[i, j] = -total_ij
+        with_unit = jnp.where(inside, jnp.where(lane == sub + first, 1.0, 0.0), block)
+        plain = [spread_row(with_unit, i) for i in range(8)]
+        rows = []
+        for i in range(8):
+            made = plain[i]
+            for e in range(i):
+                made = made + m[i, e] * plain[e]
+            rows.append(made)
+        scaled = [rows[i] * over[i] for i in range(8)]
+        solved = []
+        for i in range(8):
+            made = scaled[i]
+            for e in range(i + 1, 8):
+                made = made + m[e, i] * scaled[e]
+            solved.append(made)
+        for h in range(g + 1, 8):
+            fresh = jnp.where(inside, 0.0, a[h])
+            for i in range(8):
+                fresh = fresh - column(a[h], i) * solved[i]
+            a[h] = fresh
+        final = jnp.zeros((8, 128), F32)
+        for i in range(8):
+            final = jnp.where(sub == i, rows[i] * jnp.sqrt(over[i]), final)
+        inv.append(jnp.where(lane <= sub + first, final, 0.0))
     cross_row = jnp.where(lane[0:1] < K, total[32:33, :], 0.0)
     columns = jnp.zeros((8, 128), F32)
     weights = jnp.zeros((8, 128), F32)
@@ -338,36 +438,50 @@
     head = own.astype(jnp.bfloat16)
     tail = (own - head.astype(F32)).astype(jnp.bfloat16)
     both = jnp.concatenate([head, tail], axis=0)
+    stores = []
     for f in range(F):
         product = jnp.dot(both, split[f], preferred_element_type=F32)
         out[f] = product[0:KL] + product[KL : 2 * KL]
+        stores.append(pltpu.make_async_copy(out.at[f], out_hbm.at[:, f], bulk.at[f]))
+        stores[-1].start()
 
     joined.wait_recv()
     for t in range(2):
-        innov_out[t : t + 1, :] = part[0, t] + part[1, t]
+        innov_out[:, 128 * t : 128 * t + 128] = part[0, t] + part[1, t]
     for made in sent:
         made.wait_send()
+    for made in stores:
+        made.wait()
 
 
 def shards(
     ensemble, speed, direction, couple, obs_place, obs_field, obs_value, obs_sigma, send_count
 ):
     vmem = pl.BlockSpec(memory_space=pltpu.VMEM)
-    smem = pl.BlockSpec(memory_space=pltpu.SMEM)
+    hbm = pl.BlockSpec(memory_space=pl.ANY)
     row = lambda a: a.reshape(1, -1)
-    by_field = jnp.transpose(ensemble, (1, 0, 2)).reshape(F * KL, CELLS)
     analysis, innovation = pl.pallas_call(
         kernel,
         out_shape=(
-            jax.ShapeDtypeStruct((F, KL, CELLS), F32),
-            jax.ShapeDtypeStruct((2, 128), F32),
+            jax.ShapeDtypeStruct((KL, F, CELLS), F32),
+            jax.ShapeDtypeStruct((1, 256), F32),
         ),
-        in_specs=[vmem, vmem, vmem, smem, vmem, vmem, vmem, vmem, vmem],
-        out_specs=(vmem, vmem),
+        in_specs=[hbm] * 9,
+        out_specs=(hbm, vmem),
         scratch_shapes=[
+            pltpu.VMEM((F * KL, CELLS), F32),
+            pltpu.VMEM((F, KL, CELLS), F32),
+            pltpu.VMEM((1, CELLS), F32),
+            pltpu.VMEM((1, CELLS), I32),
+            pltpu.SMEM((F, F), F32),
+            pltpu.VMEM((1, 256), I32),
+            pltpu.VMEM((1, 256), I32),
+            pltpu.VMEM((1, 256), F32),
+            pltpu.VMEM((1, 256), F32),
+            pltpu.VMEM((1, 64), I32),
             pltpu.VMEM((F, K, CELLS), F32),
             pltpu.VMEM((F, 2 * K, CELLS), jnp.bfloat16),
-            pltpu.VMEM((3, 8, CELLS + 128), F32),
+            pltpu.VMEM((3, 8, CELLS), F32),
             pltpu.VMEM((2, 16, 128), F32),
             pltpu.VMEM((2, 16, 128), F32),
             pltpu.VMEM((128, 128), F32),
@@ -375,7 +489,6 @@
             pltpu.VMEM((4, 4, 2, 1, 128), F32),
             pltpu.VMEM((4, 4, 2, 1, 128), F32),
             pltpu.VMEM((4, 4, 4, 1, 128), F32),
-            pltpu.VMEM((3, 8, 128), F32),
             pltpu.VMEM((64, 128), I32),
             pltpu.VMEM((64, 128), I32),
             pltpu.VMEM((K, CELLS), F32),
@@ -390,16 +503,17 @@
             pltpu.VMEM((4, 40, 128), F32),
             pltpu.VMEM((2, 40, 128), F32),
             pltpu.VMEM((K, 128), F32),
-            pltpu.SemaphoreType.DMA((32,)),
-            pltpu.SemaphoreType.DMA((32,)),
+            pltpu.SemaphoreType.DMA((33,)),
+            pltpu.SemaphoreType.DMA((33,)),
             pltpu.SemaphoreType.DMA((6,)),
+            pltpu.SemaphoreType.DMA((12,)),
         ],
         compiler_params=pltpu.CompilerParams(collective_id=0, has_side_effects=True),
     )(
-        by_field, row(speed), row(direction), couple, row(obs_place), row(obs_field),
+        ensemble, row(speed), row(direction), couple, row(obs_place), row(obs_field),
         row(obs_value), row(obs_sigma), send_count,
     )
-    return jnp.transpose(analysis, (1, 0, 2)), innovation.reshape(256)
+    return analysis, innovation.reshape(256)
 
 
 def solution(mesh):

time: 54.2 us -> 42.8 us (0.79)
  Pallas kernels: 47.8 us -> 39.5 us
  local copies, waits for them, and re-layouts: 5.55 us -> 2.44 us
    pallas_call x1, Pallas kernels: 47.8 us -> 39.5 us  [shards(): pl.pallas_call(kernel, out_shape=(jax.ShapeDtypeStruct((KL, F, CELLS), F3...]
    transpose x1 -> x0, local copies, waits for them, and re-layouts: 2.14 us -> none  [shards(): by_field = jnp.transpose(ensemble, (1, 0, 2)).reshape(F * KL, CELLS)]
    unnamed x4, local copies, waits for them, and re-layouts: 3.41 us -> 2.44 us
where the time goes in v2:
time: 42.8 us; the launch traced here: 42.6 us
  Pallas kernels  39.5 us (92%)
  local copies, waits for them, and re-layouts  2.44 us (6%)
  between operations  0.65 us (2%)
    pallas_call x1, Pallas kernels, shards(): pl.pallas_call(kernel, out_shape=(jax.ShapeDtypeStruct((KL, F, CELLS), F3...  39.5 us
    unnamed x4, local copies, waits for them, and re-layouts  2.44 us

profile of v2, /device:TPU:1, one launch (start us, length us, event | category | flops | bytes accessed | tf_op | source)
XLA Modules:
  0.0 42.6 jit_solution(59777273003894207)
XLA Ops:
  0.6 39.5 %shard_map.104 = (f32[32,4,1024]{2,1,0:T(4,128)}, f32[1,256]{1,0:T(1,128)}) custom-call(f32[32,4,1024]{2,1,0:T(4,128)} %ens_hbm.1, f32[1,1024]{1,0:T(1,128)} %bitcast.7, s32[1,1024]{1,0:T(1,128)} %bitcast.8, f32[4,4]{1,0:T(4,128)} %couple_hbm.1, s32[1,256]{1,0:T(1,128)} %bitcast.9, s32[1,256]{1,0:T(1,128)} %bitcast.10, f32[1,256]{1,0:T(1,128)} %bitcast.11, ...), custom_call_target="tpu_custom_call" | custom-call | tf_op jit(solution)/shard_map/pallas_call | solution.py:463
  40.2 0.0 copy-start
  40.2 1.9 %copy.13 = f32[32,4,1024]{2,1,0:T(4,128)} copy(f32[32,4,1024]{2,1,0:T(4,128)} %get-tuple-element.8) | data formatting | bytes 1048576
  42.1 0.0 copy-done
  42.1 0.6 %copy.14 = f32[256]{0:T(256)} copy(f32[256]{0:T(256)S(1)} %bitcast.13) | data formatting | bytes 2048
Async XLA Ops:
  40.2 1.9 %copy-start = (f32[1,256]{1,0:T(1,128)S(1)}, f32[1,256]{1,0:T(1,128)}, u32[]{:S(2)}) copy-start(f32[1,256]{1,0:T(1,128)} %get-tuple-element.5) | copy-start | bytes 3076

commit v3 on v2

--- a/solution.py
+++ b/solution.py
@@ -13,6 +13,9 @@
 K = 64
 KL = 32
 CELLS = 1024
+FAR = (2, 1, 3, 0)
+PLANE = [(dx, dz) for dx in FAR for dz in FAR]
+AWAY = [(dx, dz, dy) for dy in FAR for dx, dz in PLANE if dx or dz or dy]
 HALF = 16
 F32 = jnp.float32
 I32 = jnp.int32
@@ -28,30 +31,26 @@
     counts_hbm, out_hbm, innov_out,
     ens, out, speed, direction, couple, place, field, value, sigma, counts,
     states, split, coef, halo_out, halo_in, edge,
-    m0, m1, m2, m3, starts_s, counts_s, picked, innov_s,
-    n0, n1, n2, n3, part, gy, gz, gx, gc, mix, send, recv, local, bulk,
+    m0, m3, starts_s, counts_s, picked, innov_s,
+    n0, n3, part, gp, gy, gc, mix, send, recv, bulk,
+    ask_send, ask_recv, back_send, back_recv, plane_send, plane_recv,
 ):
     cells = lax.axis_index("cells")
     core = lax.axis_index("members")
-    x = cells % 4
-    z = (cells // 4) % 4
+    x = lax.rem(cells, 4)
+    z = lax.rem(cells // 4, 4)
     y = cells // 16
-    left_id = (cells + 63) % 64
-    right_id = (cells + 1) % 64
-    axes = {"x": (x, 1), "z": (z, 4), "y": (y, 16)}
-
-    def peer(axis, step):
-        mine, stride = axes[axis]
-        other = (mine + step) % 4
-        return other, {"cells": cells + (other - mine) * stride, "members": core}
+    left_id = lax.rem(cells + 63, 64)
+    right_id = lax.rem(cells + 1, 64)
+    pair_id = {"cells": cells, "members": 1 - core}
+    xs = [lax.rem(x + d, 4) for d in range(4)]
+    zs = [lax.rem(z + d, 4) for d in range(4)]
+    ys = [lax.rem(y + d, 4) for d in range(4)]
+    half_row = [t // 2 for t in ys]
+    in_plane = {(dx, dz): zs[dz] * 4 + xs[dx] for dx, dz in PLANE}
+    asked_row = {(dx, dz): xs[dx] * 8 + zs[dz] * 2 for dx, dz in PLANE}
 
     barrier = pltpu.get_barrier_semaphore()
-    for axis in ("x", "z", "y"):
-        for step in (1, 2, 3):
-            pl.semaphore_signal(barrier, inc=1, device_id=peer(axis, step)[1])
-    pl.semaphore_signal(barrier, inc=1, device_id={"cells": cells, "members": 1 - core})
-    pl.semaphore_signal(barrier, inc=1, device_id={"cells": left_id, "members": core})
-    pl.semaphore_signal(barrier, inc=1, device_id={"cells": right_id, "members": core})
 
     small = (
         (counts_hbm, counts), (place_hbm, place), (field_hbm, field), (value_hbm, value),
@@ -61,15 +60,18 @@
     loads = [
         pltpu.make_async_copy(ens_hbm.at[:, f], ens.at[pl.ds(f * KL, KL)], bulk.at[f]) for f in range(F)
     ]
-    for made in early + loads:
+    for made in early:
         made.start()
-
-    used = [0, 0]
+    for dx, dz, dy in AWAY:
+        target = ys[dy] * 16 + in_plane[dx, dz]
+        pl.semaphore_signal(barrier, inc=1, device_id={"cells": target, "members": core})
+    pl.semaphore_signal(barrier, inc=1, device_id=pair_id)
+    for made in loads:
+        made.start()
+
     sent = []
 
-    def copy_to(src, dst, device):
-        at = used[0]
-        used[0] += 1
+    def copy_to(src, dst, at, device):
         made = pltpu.make_async_remote_copy(
             src_ref=src, dst_ref=dst, send_sem=send.at[at], recv_sem=recv.at[at], device_id=device
         )
@@ -77,17 +79,8 @@
         sent.append(made)
         return made
 
-    def copy_here(src, dst):
-        at = used[1]
-        used[1] += 1
-        made = pltpu.make_async_copy(src, dst, local.at[at])
-        made.start()
-        return made
-
-    def arrive(copies):
-        for made in copies[:-1]:
-            made.wait_recv()
-        copies[-1].wait()
+    def whole(ref, sem):
+        return pltpu.make_async_copy(ref, ref, sem)
 
     lane = lax.broadcasted_iota(I32, (8, 128), 1)
     sub = lax.broadcasted_iota(I32, (8, 128), 0)
@@ -129,10 +122,10 @@
             got = jnp.where(second, lanes_of(tables[q][1], low), lanes_of(tables[q][0], low))
             found = jnp.where(which == q, got, found)
         found = jnp.where(rank < number, found, 0.0)
-        m0[g] = found.reshape(4, 2, 1, 128)
+        m0[8 * g : 8 * g + 8] = found.reshape(8, 1, 128)
     for g in range(8):
         row = sub64 + 8 * g
-        begin, number = start_and_count(row % 4 * 16 + (row // 4) % 4 * 4 + row // 16)
+        begin, number = start_and_count(row)
         starts_s[8 * g : 8 * g + 8, :] = jnp.broadcast_to(begin, (8, 128))
         counts_s[8 * g : 8 * g + 8, :] = jnp.broadcast_to(number, (8, 128))
 
@@ -146,18 +139,21 @@
         halo_out[side, 9:10, :] = toward_left[:, first : first + 128]
         halo_out[side, 10:16, :] = jnp.zeros((6, 128), F32)
 
-    pl.semaphore_wait(barrier, 12)
-
+    pl.semaphore_wait(barrier, 64)
+
+    for dx, dz, dy in AWAY:
+        target = ys[dy] * 16 + in_plane[dx, dz]
+        pltpu.make_async_remote_copy(
+            src_ref=m0.at[asked_row[dx, dz] + half_row[dy]], dst_ref=m3.at[cells],
+            send_sem=ask_send.at[0], recv_sem=ask_recv.at[cells // 8],
+            device_id={"cells": target, "members": core},
+        ).start()
+    own_row = asked_row[0, 0] + half_row[0]
+    pltpu.make_async_copy(m0.at[own_row], m3.at[cells], ask_recv.at[cells // 8]).start()
     halo = [
-        copy_to(halo_out.at[0], halo_in.at[0], {"cells": right_id, "members": core}),
-        copy_to(halo_out.at[1], halo_in.at[1], {"cells": left_id, "members": core}),
+        copy_to(halo_out.at[0], halo_in.at[0], 0, {"cells": right_id, "members": core}),
+        copy_to(halo_out.at[1], halo_in.at[1], 1, {"cells": left_id, "members": core}),
     ]
-
-    def exchange(axis, src_of, dst):
-        made = [copy_to(src_of(peer(axis, s)[0]), dst, peer(axis, s)[1]) for s in (1, 2, 3)]
-        return made + [copy_here(src_of(axes[axis][0]), dst)]
-
-    going = exchange("x", lambda o: m0.at[o], m1.at[x])
 
     gain = [[couple[f, g] + (1.0 if f == g else 0.0) for g in range(F)] for f in range(F)]
     for _ in range(2):
@@ -197,9 +193,6 @@
         return carry
 
     lax.fori_loop(0, 4, interior, 0)
-
-    arrive(going)
-    going = exchange("z", lambda o: m1.at[:, o], m2.at[z])
 
     for made in halo:
         made.wait_recv()
@@ -240,83 +233,93 @@
     lax.fori_loop(0, 4, border, 0)
 
     mine = states.at[:, pl.ds(pl.multiple_of(core * KL, KL), KL), :]
-    swap = copy_to(mine, mine, {"cells": cells, "members": 1 - core})
-
-    arrive(going)
-    base = used[0]
-    used[0] += 4
-    own_rows = pltpu.make_async_copy(m2.at[:, :, y // 2], m3.at[y], recv.at[base])
-    own_rows.start()
-    for step in (1, 3, 2):
-        o, device = peer("y", step)
-        made = pltpu.make_async_remote_copy(
-            src_ref=m2.at[:, :, o // 2], dst_ref=m3.at[y],
-            send_sem=send.at[base + step], recv_sem=recv.at[base + step], device_id=device,
-        )
-        made.start()
-        sent.append(made)
+    swap = copy_to(mine, mine, 2, pair_id)
+
     swap.wait_recv()
 
-    off = (y % 2) * 64
-
-    def pick(turn, carry):
-        t = turn // 2
+    off = lax.rem(y, 2) * 64
+
+    def answer(r):
+        for i in range(8):
+            source = 8 * r + i
+
+            @pl.when(source != cells)
+            def _():
+                pltpu.make_async_remote_copy(
+                    src_ref=n0.at[r], dst_ref=n3.at[cells], send_sem=back_send.at[0],
+                    recv_sem=back_recv.at[0], device_id={"cells": source, "members": core},
+                ).start()
+
+            @pl.when(source == cells)
+            def _():
+                pltpu.make_async_copy(n0.at[r], n3.at[cells], back_recv.at[0]).start()
+
+    def plane_at(t):
         step = t + t // 2 - 2 * (t // 3)
-        source = (y + 4 - step) % 4
-        pair = turn % 2
-        r = source * 2 + pair
-
-        @pl.when(pair == 0)
+        return lax.rem(y + 4 - step, 4)
+
+    def pick(t, carry):
+        plane = plane_at(t)
+
+        @pl.when(t > 0)
         def _():
-            pltpu.make_async_copy(m3.at[source], m3.at[source], recv.at[base + step]).wait()
-
-        rows = m3[source, pl.ds(2 * pair, 2)].reshape(8, 128)
+            before = plane_at(t - 1)
+            answer(2 * before)
+            answer(2 * before + 1)
+
         asked = []
-        for q in range(3):
-            got = lanes_of(rows, off + 16 * q + slot)
-            got = jnp.where(lane // 16 == sub, got, 0.0)
-            asked.append(jnp.sum(got, axis=0, keepdims=True))
-        index = jnp.broadcast_to(asked[0], (8, 128)).astype(I32)
-        low = index & 127
-        high = index // 128
-        found = [jnp.zeros((8, 128), F32)] * 8
-        for c in range(32):
-            here = high == c
+        for pair in range(2):
+            r = 2 * plane + pair
+            rows_ref = m3.at[pl.ds(8 * r, 8)]
+            whole(rows_ref, ask_recv.at[r]).wait()
+            rows = m3[pl.ds(8 * r, 8)].reshape(8, 128)
+            for q in range(3):
+                got = lanes_of(rows, off + 16 * q + slot)
+                got = jnp.where(lane // 16 == sub, got, 0.0)
+                asked.append(jnp.sum(got, axis=0, keepdims=True))
+        for pair in range(2):
+            r = 2 * plane + pair
+            index, observed, scale = asked[3 * pair : 3 * pair + 3]
+            index = jnp.broadcast_to(index, (8, 128)).astype(I32)
+            low = index & 127
+            high = index // 128
+            found = [jnp.zeros((8, 128), F32)] * 8
+            for c in range(32):
+                here = high == c
+                for g in range(8):
+                    tile = states[c // 8, 8 * g : 8 * g + 8, (c % 8) * 128 : (c % 8) * 128 + 128]
+                    found[g] = jnp.where(here, lanes_of(tile, low), found[g])
+            total = found[0]
+            for g in range(1, 8):
+                total = total + found[g]
+            center = jnp.sum(total, axis=0, keepdims=True) / K
+            at = pl.ds(pl.multiple_of(r * 128, 128), 128)
             for g in range(8):
-                tile = states[c // 8, 8 * g : 8 * g + 8, (c % 8) * 128 : (c % 8) * 128 + 128]
-                found[g] = jnp.where(here, lanes_of(tile, low), found[g])
-        total = found[0]
-        for g in range(1, 8):
-            total = total + found[g]
-        center = jnp.sum(total, axis=0, keepdims=True) / K
-        at = pl.ds(pl.multiple_of(r * 128, 128), 128)
-        for g in range(8):
-            picked[8 * g : 8 * g + 8, at] = (found[g] - center) * asked[2]
-        row = (asked[1] - center) * asked[2]
-        innov_s[:, at] = jnp.where(sub == 0, row, 0.0)
-        n0[r] = row
+                picked[8 * g : 8 * g + 8, at] = (found[g] - center) * scale
+            row = (observed - center) * scale
+            innov_s[:, at] = jnp.where(sub == 0, row, 0.0)
+            n0[r] = row
         return carry
 
-    lax.fori_loop(0, 8, pick, 0)
+    lax.fori_loop(0, 4, pick, 0)
 
     contract = (((1,), (1,)), ((), ()))
     anomalies = picked[...]
     gram = lax.dot_general(anomalies, anomalies, contract, precision=HIGHEST, preferred_element_type=F32)
     cross = lax.dot_general(innov_s[...], anomalies, contract, precision=HIGHEST, preferred_element_type=F32)
-    gy[y, 0:32, :] = jnp.concatenate([gram[0:32], gram[32:64]], axis=1)
-    gy[y, 32:40, :] = jnp.concatenate([cross, jnp.zeros((8, 64), F32)], axis=1)
-
-    def share(axis, ref):
-        at = axes[axis][0]
-        return [copy_to(ref.at[at], ref.at[at], peer(axis, s)[1]) for s in (1, 2, 3)]
-
-    def collect(copies, ref):
-        for made in copies:
-            made.wait_recv()
-        return (ref[0] + ref[1]) + (ref[2] + ref[3])
-
-    adding = share("y", gy)
-    back = exchange("y", lambda o: n0.at[pl.ds(2 * o, 2)], n1.at[y])
+    here = z * 4 + x
+    gp[here, 0:32, :] = jnp.concatenate([gram[0:32], gram[32:64]], axis=1)
+    gp[here, 32:40, :] = jnp.concatenate([cross, jnp.zeros((8, 64), F32)], axis=1)
+
+    for dx, dz in PLANE[:-1]:
+        target = y * 16 + in_plane[dx, dz]
+        pltpu.make_async_remote_copy(
+            src_ref=gp.at[here], dst_ref=gp.at[here], send_sem=plane_send.at[0],
+            recv_sem=plane_recv.at[0], device_id={"cells": target, "members": core},
+        ).start()
+    last = plane_at(3)
+    answer(2 * last)
+    answer(2 * last + 1)
 
     for f in range(F):
         full = states[f]
@@ -324,24 +327,25 @@
         split[f, 0:K, :] = head
         split[f, K : 2 * K, :] = (full - head.astype(F32)).astype(jnp.bfloat16)
 
-    gz[z] = collect(adding, gy)
-    adding = share("z", gz)
-    arrive(back)
-    back = exchange("z", lambda o: n1.at[:, o // 2], n2.at[z])
-
-    gx[x] = collect(adding, gz)
-    adding = share("x", gx)
-    arrive(back)
-    back = exchange("x", lambda o: n2, n3.at[x])
-
-    gc[core] = collect(adding, gx)
-    adding = copy_to(gc.at[core], gc.at[core], {"cells": cells, "members": 1 - core})
-
-    arrive(back)
-    shift = 64 * (z % 2) + 16 * x - HALF * core
+    whole(gp.at[pl.ds(0, 15)], plane_recv.at[0]).wait()
+    total = gp[0]
+    for i in range(1, 16):
+        total = total + gp[i]
+    gy[y] = total
+    adding = [
+        copy_to(gy.at[y], gy.at[y], 3 + step, {"cells": ys[step] * 16 + here, "members": core})
+        for step in (2, 1, 3)
+    ]
+    for made in adding:
+        made.wait_recv()
+    gc[core] = (gy[0] + gy[1]) + (gy[2] + gy[3])
+    adding = copy_to(gc.at[core], gc.at[core], 3, pair_id)
+
+    whole(n3, back_recv.at[0]).wait()
+    shift = 16 * lax.rem(cells, 8) - HALF * core
     totals = [jnp.zeros((8, 128), F32)] * 2
     for g in range(8):
-        rows = n3[g // 2, 2 * (g % 2) : 2 * (g % 2) + 2].reshape(8, 128)
+        rows = n3[8 * g : 8 * g + 8].reshape(8, 128)
         begin = starts_s[8 * g : 8 * g + 8, :]
         number = counts_s[8 * g : 8 * g + 8, :]
         for t in range(2):
@@ -352,7 +356,7 @@
             totals[t] = totals[t] + jnp.where(good, got, 0.0)
     for t in range(2):
         part[core, t] = jnp.sum(totals[t], axis=0, keepdims=True)
-    joined = copy_to(part.at[core], part.at[core], {"cells": cells, "members": 1 - core})
+    joined = copy_to(part.at[core], part.at[core], 7, pair_id)
 
     adding.wait_recv()
     total = gc[0] + gc[1]
@@ -450,6 +454,10 @@
         innov_out[:, 128 * t : 128 * t + 128] = part[0, t] + part[1, t]
     for made in sent:
         made.wait_send()
+    for ref, sem in (
+        (m3.at[pl.ds(0, 63)], ask_send), (n3.at[pl.ds(0, 63)], back_send), (gp.at[pl.ds(0, 15)], plane_send),
+    ):
+        whole(ref, sem.at[0]).wait()
     for made in stores:
         made.wait()
 
@@ -485,28 +493,28 @@
             pltpu.VMEM((2, 16, 128), F32),
             pltpu.VMEM((2, 16, 128), F32),
             pltpu.VMEM((128, 128), F32),
-            pltpu.VMEM((4, 4, 2, 1, 128), F32),
-            pltpu.VMEM((4, 4, 2, 1, 128), F32),
-            pltpu.VMEM((4, 4, 2, 1, 128), F32),
-            pltpu.VMEM((4, 4, 4, 1, 128), F32),
+            pltpu.VMEM((32, 1, 128), F32),
+            pltpu.VMEM((64, 1, 128), F32),
             pltpu.VMEM((64, 128), I32),
             pltpu.VMEM((64, 128), I32),
             pltpu.VMEM((K, CELLS), F32),
             pltpu.VMEM((8, CELLS), F32),
             pltpu.VMEM((8, 1, 128), F32),
-            pltpu.VMEM((4, 2, 1, 128), F32),
-            pltpu.VMEM((4, 4, 1, 128), F32),
-            pltpu.VMEM((4, 4, 4, 1, 128), F32),
+            pltpu.VMEM((64, 1, 128), F32),
             pltpu.VMEM((2, 2, 1, 128), F32),
-            pltpu.VMEM((4, 40, 128), F32),
-            pltpu.VMEM((4, 40, 128), F32),
+            pltpu.VMEM((16, 40, 128), F32),
             pltpu.VMEM((4, 40, 128), F32),
             pltpu.VMEM((2, 40, 128), F32),
             pltpu.VMEM((K, 128), F32),
-            pltpu.SemaphoreType.DMA((33,)),
-            pltpu.SemaphoreType.DMA((33,)),
-            pltpu.SemaphoreType.DMA((6,)),
+            pltpu.SemaphoreType.DMA((8,)),
+            pltpu.SemaphoreType.DMA((8,)),
             pltpu.SemaphoreType.DMA((12,)),
+            pltpu.SemaphoreType.DMA((1,)),
+            pltpu.SemaphoreType.DMA((8,)),
+            pltpu.SemaphoreType.DMA((1,)),
+            pltpu.SemaphoreType.DMA((1,)),
+            pltpu.SemaphoreType.DMA((1,)),
+            pltpu.SemaphoreType.DMA((1,)),
         ],
         compiler_params=pltpu.CompilerParams(collective_id=0, has_side_effects=True),
     )(

time: 42.8 us -> 38.8 us (0.907)
  Pallas kernels: 39.5 us -> 35.6 us
    pallas_call x1, Pallas kernels: 39.5 us -> 35.6 us  [shards(): pl.pallas_call(kernel, out_shape=(jax.ShapeDtypeStruct((KL, F, CELLS), F3...]
where the time goes in v3:
time: 38.8 us; the launch traced here: 38.6 us
  Pallas kernels  35.6 us (92%)
  local copies, waits for them, and re-layouts  2.44 us (6%)
  between operations  0.65 us (2%)
    pallas_call x1, Pallas kernels, shards(): pl.pallas_call(kernel, out_shape=(jax.ShapeDtypeStruct((KL, F, CELLS), F3...  35.6 us
    unnamed x4, local copies, waits for them, and re-layouts  2.44 us

profile of v3, /device:TPU:1, one launch (start us, length us, event | category | flops | bytes accessed | tf_op | source)
XLA Modules:
  0.0 38.6 jit_solution(6303236223669210962)
XLA Ops:
  0.6 35.6 %shard_map.104 = (f32[32,4,1024]{2,1,0:T(4,128)}, f32[1,256]{1,0:T(1,128)}) custom-call(f32[32,4,1024]{2,1,0:T(4,128)} %ens_hbm.1, f32[1,1024]{1,0:T(1,128)} %bitcast.7, s32[1,1024]{1,0:T(1,128)} %bitcast.8, f32[4,4]{1,0:T(4,128)} %couple_hbm.1, s32[1,256]{1,0:T(1,128)} %bitcast.9, s32[1,256]{1,0:T(1,128)} %bitcast.10, f32[1,256]{1,0:T(1,128)} %bitcast.11, ...), custom_call_target="tpu_custom_call" | custom-call | tf_op jit(solution)/shard_map/pallas_call | solution.py:471
  36.2 0.0 copy-start
  36.2 1.9 %copy.13 = f32[32,4,1024]{2,1,0:T(4,128)} copy(f32[32,4,1024]{2,1,0:T(4,128)} %get-tuple-element.8) | data formatting | bytes 1048576
  38.1 0.0 copy-done
  38.1 0.6 %copy.14 = f32[256]{0:T(256)} copy(f32[256]{0:T(256)S(1)} %bitcast.13) | data formatting | bytes 2048
Async XLA Ops:
  36.2 1.9 %copy-start = (f32[1,256]{1,0:T(1,128)S(1)}, f32[1,256]{1,0:T(1,128)}, u32[]{:S(2)}) copy-start(f32[1,256]{1,0:T(1,128)} %get-tuple-element.5) | copy-start | bytes 3076

commit v4 on v3

--- a/solution.py
+++ b/solution.py
@@ -28,12 +28,12 @@
 
 def kernel(
     ens_hbm, speed_hbm, direction_hbm, couple_hbm, place_hbm, field_hbm, value_hbm, sigma_hbm,
-    counts_hbm, out_hbm, innov_out,
-    ens, out, speed, direction, couple, place, field, value, sigma, counts,
-    states, split, coef, halo_out, halo_in, edge,
-    m0, m3, starts_s, counts_s, picked, innov_s,
-    n0, n3, part, gp, gy, gc, mix, send, recv, bulk,
-    ask_send, ask_recv, back_send, back_recv, plane_send, plane_recv,
+    counts_hbm, out, innov_out,
+    ens, speed, direction, couple, place, field, value, sigma, counts,
+    states, split, coef, halo_out, halo_in, edge, base, keep, places, raw,
+    m0, m3, starts_s, counts_s, gram_s, cross_s,
+    n0, n3, part, g1, g2, gc, mix, send, recv, bulk,
+    ask_send, ask_recv, back_send, back_recv, plane_send, plane_recv, halo_send, halo_recv,
 ):
     cells = lax.axis_index("cells")
     core = lax.axis_index("members")
@@ -52,6 +52,12 @@
 
     barrier = pltpu.get_barrier_semaphore()
 
+    for dx, dz, dy in AWAY:
+        target = ys[dy] * 16 + in_plane[dx, dz]
+        pl.semaphore_signal(barrier, inc=1, device_id={"cells": target, "members": core})
+    pl.semaphore_signal(barrier, inc=1, device_id=pair_id)
+    for neighbour in (left_id, right_id):
+        pl.semaphore_signal(barrier, inc=1, device_id={"cells": neighbour, "members": 1 - core})
     small = (
         (counts_hbm, counts), (place_hbm, place), (field_hbm, field), (value_hbm, value),
         (sigma_hbm, sigma), (speed_hbm, speed), (direction_hbm, direction), (couple_hbm, couple),
@@ -62,10 +68,6 @@
     ]
     for made in early:
         made.start()
-    for dx, dz, dy in AWAY:
-        target = ys[dy] * 16 + in_plane[dx, dz]
-        pl.semaphore_signal(barrier, inc=1, device_id={"cells": target, "members": core})
-    pl.semaphore_signal(barrier, inc=1, device_id=pair_id)
     for made in loads:
         made.start()
 
@@ -108,9 +110,9 @@
     upper = lane >= 64
     for g in range(4):
         row = sub64 + 8 * g
-        base = (row // 2) % 4 * 4 + row // 8 + (row % 2) * 32
-        b0, c0 = start_and_count(base)
-        b1, c1 = start_and_count(base + 16)
+        lower = (row // 2) % 4 * 4 + row // 8 + (row % 2) * 32
+        b0, c0 = start_and_count(lower)
+        b1, c1 = start_and_count(lower + 16)
         begin = jnp.where(upper, b1, b0)
         number = jnp.where(upper, c1, c0)
         rank = slot + HALF * core
@@ -138,23 +140,15 @@
         halo_out[side, 8:9, :] = speed[:, first : first + 128]
         halo_out[side, 9:10, :] = toward_left[:, first : first + 128]
         halo_out[side, 10:16, :] = jnp.zeros((6, 128), F32)
-
-    pl.semaphore_wait(barrier, 64)
-
-    for dx, dz, dy in AWAY:
-        target = ys[dy] * 16 + in_plane[dx, dz]
-        pltpu.make_async_remote_copy(
-            src_ref=m0.at[asked_row[dx, dz] + half_row[dy]], dst_ref=m3.at[cells],
-            send_sem=ask_send.at[0], recv_sem=ask_recv.at[cells // 8],
-            device_id={"cells": target, "members": core},
-        ).start()
-    own_row = asked_row[0, 0] + half_row[0]
-    pltpu.make_async_copy(m0.at[own_row], m3.at[cells], ask_recv.at[cells // 8]).start()
-    halo = [
-        copy_to(halo_out.at[0], halo_in.at[0], 0, {"cells": right_id, "members": core}),
-        copy_to(halo_out.at[1], halo_in.at[1], 1, {"cells": left_id, "members": core}),
-    ]
-
+    wide = lax.broadcasted_iota(I32, (F * KL, 128), 1)
+    base[core] = jnp.where(wide < 32, ens[:, 0:128], pltpu.roll(ens[:, CELLS - 128 :], 64, 1))
+
+    for m in range(2):
+        edge[m] = jnp.zeros((128, 128), F32)
+    gram_s[...] = jnp.zeros((K, K), F32)
+    cross_s[...] = jnp.zeros((K, 128), F32)
+    keep[...] = jnp.zeros((2, 8, 128), F32)
+    raw[...] = jnp.zeros((2, K, 256), F32)
     gain = [[couple[f, g] + (1.0 if f == g else 0.0) for g in range(F)] for f in range(F)]
     for _ in range(2):
         gain = [
@@ -192,50 +186,75 @@
             states[f, into, :] = made
         return carry
 
-    lax.fori_loop(0, 4, interior, 0)
-
-    for made in halo:
-        made.wait_recv()
+    lax.fori_loop(0, 2, interior, 0)
+
+    pl.semaphore_wait(barrier, 66)
+
+    for to in range(2):
+        for side, neighbour in ((0, right_id), (1, left_id)):
+            pltpu.make_async_remote_copy(
+                src_ref=halo_out.at[side], dst_ref=halo_in.at[side, core],
+                send_sem=halo_send.at[0], recv_sem=halo_recv.at[0],
+                device_id={"cells": neighbour, "members": to},
+            ).start()
+    based = copy_to(base.at[core], base.at[core], 0, pair_id)
+    for dx, dz, dy in AWAY:
+        target = ys[dy] * 16 + in_plane[dx, dz]
+        pltpu.make_async_remote_copy(
+            src_ref=m0.at[asked_row[dx, dz] + half_row[dy]], dst_ref=m3.at[cells],
+            send_sem=ask_send.at[0], recv_sem=ask_recv.at[cells // 8],
+            device_id={"cells": target, "members": core},
+        ).start()
+    own_row = asked_row[0, 0] + half_row[0]
+    pltpu.make_async_copy(m0.at[own_row], m3.at[cells], ask_recv.at[cells // 8]).start()
+    lax.fori_loop(2, 4, interior, 0)
+
+    mine = states.at[:, pl.ds(pl.multiple_of(core * KL, KL), KL), :]
+    swap = copy_to(mine, mine, 2, pair_id)
+
+    based.wait_recv()
+    whole(halo_in, halo_recv.at[0]).wait()
+    swap.wait()
     has_left = jnp.where(cells > 0, 1.0, 0.0).astype(F32)
     has_right = jnp.where(cells < 63, 1.0, 0.0).astype(F32)
-    present = jnp.where(lane < 64, has_right, has_left)
-    edge[0:8, :] = halo_in[1, 0:8, :] * has_right
-    edge[8:120, :] = jnp.zeros((112, 128), F32)
-    edge[120:128, :] = halo_in[0, 0:8, :] * has_left
-    edge[...] = jnp.transpose(edge[...])
-    edge_speed = jnp.where(lane < 64, halo_in[1, 8:9, :], halo_in[0, 8:9, :])
-    edge_left = jnp.where(lane < 64, halo_in[1, 9:10, :], halo_in[0, 9:10, :])
+    for m in range(2):
+        edge[m, 64:72, :] = halo_in[1, m, 0:8, :] * has_right
+        edge[m, 120:128, :] = halo_in[0, m, 0:8, :] * has_left
+        edge[m] = jnp.where(wide < 64, base[m], jnp.transpose(edge[m]))
+    beyond = lane < 96
+    present = jnp.where(beyond, has_right, has_left)
+
+    def outside(row):
+        after = jnp.broadcast_to(halo_in[1, 0, row : row + 1, :], (8, 128))
+        before = jnp.broadcast_to(halo_in[0, 0, row : row + 1, :], (8, 128))
+        return jnp.where(beyond, pltpu.roll(after, 64, 1), before)
+
+    edge_speed, edge_left = outside(8), outside(9)
     around = (
         present * (1.0 - 2.0 * DIFFUSION - edge_speed),
         present * (edge_left + DIFFUSION),
         present * (edge_speed - edge_left + DIFFUSION),
     )
-    strip = [
-        jnp.concatenate([coef[i, :, CELLS - 128 :], around[i], coef[i, :, 0:128]], axis=1)
-        for i in range(3)
-    ]
-
-    def border(group, carry):
-        rows = pl.multiple_of(group * 8, 8)
-        into = pl.ds(pl.multiple_of(core * KL + rows, 8), 8)
-        moved = []
-        for f in range(F):
-            at = pl.ds(f * KL + rows, 8)
-            u = jnp.concatenate([ens[at, CELLS - 128 :], edge[at, :], ens[at, 0:128]], axis=1)
-            moved.append(transport(u, *strip))
-        for f, made in enumerate(coupled(moved)):
-            before = states[f, into, CELLS - 128 :]
-            states[f, into, CELLS - 128 :] = jnp.where(lane >= 64, made[:, 0:128], before)
-            after = states[f, into, 0:128]
-            states[f, into, 0:128] = jnp.where(lane < 64, made[:, 256:384], after)
+    strip = []
+    for i in range(3):
+        inner = jnp.where(lane < 32, coef[i, :, 0:128], pltpu.roll(coef[i, :, CELLS - 128 :], 64, 1))
+        strip.append(jnp.where(lane < 64, inner, around[i]))
+
+    def border(m, carry):
+        for group in range(4):
+            into = pl.ds(pl.multiple_of(m * KL + 8 * group, 8), 8)
+            moved = [
+                transport(edge[m, f * KL + 8 * group : f * KL + 8 * group + 8, :], *strip)
+                for f in range(F)
+            ]
+            for f, made in enumerate(coupled(moved)):
+                first = states[f, into, 0:128]
+                states[f, into, 0:128] = jnp.where(lane < 4, made, first)
+                last = states[f, into, CELLS - 128 :]
+                states[f, into, CELLS - 128 :] = jnp.where(lane >= 124, pltpu.roll(made, 64, 1), last)
         return carry
 
-    lax.fori_loop(0, 4, border, 0)
-
-    mine = states.at[:, pl.ds(pl.multiple_of(core * KL, KL), KL), :]
-    swap = copy_to(mine, mine, 2, pair_id)
-
-    swap.wait_recv()
+    lax.fori_loop(0, 2, border, 0)
 
     off = lax.rem(y, 2) * 64
 
@@ -258,29 +277,66 @@
         step = t + t // 2 - 2 * (t // 3)
         return lax.rem(y + 4 - step, 4)
 
-    def pick(t, carry):
-        plane = plane_at(t)
-
-        @pl.when(t > 0)
-        def _():
-            before = plane_at(t - 1)
-            answer(2 * before)
-            answer(2 * before + 1)
-
-        asked = []
+    def finish(plane, turn):
+        anomalies = [[] for _ in range(8)]
+        crossed = [cross_s[8 * g : 8 * g + 8, :] for g in range(8)]
         for pair in range(2):
             r = 2 * plane + pair
-            rows_ref = m3.at[pl.ds(8 * r, 8)]
-            whole(rows_ref, ask_recv.at[r]).wait()
-            rows = m3[pl.ds(8 * r, 8)].reshape(8, 128)
+            found = [raw[turn, 8 * g : 8 * g + 8, 128 * pair : 128 * pair + 128] for g in range(8)]
+            total = found[0]
+            for g in range(1, 8):
+                total = total + found[g]
+            center = jnp.sum(total, axis=0, keepdims=True) / K
+            observed = keep[turn, pair : pair + 1, :]
+            scale = keep[turn, 2 + pair : 3 + pair, :]
+            row = (observed - center) * scale
+            n0[r] = row
+            for g in range(8):
+                made = (found[g] - center) * scale
+                anomalies[g].append(made)
+                crossed[g] = crossed[g] + made * row
+        stacked = jnp.concatenate([jnp.concatenate(a, axis=1) for a in anomalies], axis=0)
+        gram_s[...] += lax.dot_general(
+            stacked, stacked, (((1,), (1,)), ((), ())), precision=HIGHEST, preferred_element_type=F32
+        )
+        for g in range(8):
+            cross_s[8 * g : 8 * g + 8, :] = crossed[g]
+
+    def arrived(plane):
+        for pair in range(2):
+            r = 2 * plane + pair
+            whole(m3.at[pl.ds(8 * r, 8)], ask_recv.at[r]).wait()
+
+    def prepare(plane, turn):
+        for pair in range(2):
+            rows = m3[pl.ds(8 * (2 * plane + pair), 8)].reshape(8, 128)
+            asked = []
             for q in range(3):
                 got = lanes_of(rows, off + 16 * q + slot)
                 got = jnp.where(lane // 16 == sub, got, 0.0)
                 asked.append(jnp.sum(got, axis=0, keepdims=True))
+            places[pair : pair + 1, :] = asked[0]
+            keep[turn, pair : pair + 1, :] = asked[1]
+            keep[turn, 2 + pair : 3 + pair, :] = asked[2]
+
+    def pick(t, carry):
+        turn = lax.rem(t, 2)
+
+        @pl.when(t > 1)
+        def _():
+            before = plane_at(t - 2)
+            answer(2 * before)
+            answer(2 * before + 1)
+
+        @pl.when(t < 3)
+        def _():
+            arrived(plane_at(t + 1))
+
+        finish(plane_at(lax.rem(t + 3, 4)), 1 - turn)
+        indices = [places[pair : pair + 1, :] for pair in range(2)]
+        prepare(plane_at(lax.rem(t + 1, 4)), 1 - turn)
         for pair in range(2):
-            r = 2 * plane + pair
-            index, observed, scale = asked[3 * pair : 3 * pair + 3]
-            index = jnp.broadcast_to(index, (8, 128)).astype(I32)
+            index = jnp.broadcast_to(indices[pair], (8, 128)).astype(I32)
             low = index & 127
             high = index // 128
             found = [jnp.zeros((8, 128), F32)] * 8
@@ -289,37 +345,35 @@
                 for g in range(8):
                     tile = states[c // 8, 8 * g : 8 * g + 8, (c % 8) * 128 : (c % 8) * 128 + 128]
                     found[g] = jnp.where(here, lanes_of(tile, low), found[g])
-            total = found[0]
-            for g in range(1, 8):
-                total = total + found[g]
-            center = jnp.sum(total, axis=0, keepdims=True) / K
-            at = pl.ds(pl.multiple_of(r * 128, 128), 128)
             for g in range(8):
-                picked[8 * g : 8 * g + 8, at] = (found[g] - center) * scale
-            row = (observed - center) * scale
-            innov_s[:, at] = jnp.where(sub == 0, row, 0.0)
-            n0[r] = row
+                raw[turn, 8 * g : 8 * g + 8, 128 * pair : 128 * pair + 128] = found[g]
         return carry
 
+    arrived(y)
+    prepare(y, 0)
     lax.fori_loop(0, 4, pick, 0)
-
-    contract = (((1,), (1,)), ((), ()))
-    anomalies = picked[...]
-    gram = lax.dot_general(anomalies, anomalies, contract, precision=HIGHEST, preferred_element_type=F32)
-    cross = lax.dot_general(innov_s[...], anomalies, contract, precision=HIGHEST, preferred_element_type=F32)
-    here = z * 4 + x
-    gp[here, 0:32, :] = jnp.concatenate([gram[0:32], gram[32:64]], axis=1)
-    gp[here, 32:40, :] = jnp.concatenate([cross, jnp.zeros((8, 64), F32)], axis=1)
-
-    for dx, dz in PLANE[:-1]:
-        target = y * 16 + in_plane[dx, dz]
+    finish(plane_at(3), 1)
+
+    cross = jnp.sum(cross_s[...], axis=1, keepdims=True)
+    gram = gram_s[...]
+    apart = lax.broadcasted_iota(I32, (32, 64), 1)
+    lower = jnp.where(
+        apart >= 32, gram[32:64],
+        jnp.where(apart == 0, cross[0:32], jnp.where(apart == 1, cross[32:64], 0.0)),
+    )
+    first_at = lax.rem(y, 2) * 4 + x
+    g1[first_at] = jnp.concatenate([gram[0:32], lower], axis=1)
+
+    beside = y + 1 - 2 * lax.rem(y, 2)
+    for across, dx in ((1, 2), (0, 2), (1, 1), (1, 3), (0, 1), (0, 3), (1, 0)):
+        target = (beside if across else y) * 16 + z * 4 + xs[dx]
         pltpu.make_async_remote_copy(
-            src_ref=gp.at[here], dst_ref=gp.at[here], send_sem=plane_send.at[0],
+            src_ref=g1.at[first_at], dst_ref=g1.at[first_at], send_sem=plane_send.at[0],
             recv_sem=plane_recv.at[0], device_id={"cells": target, "members": core},
         ).start()
-    last = plane_at(3)
-    answer(2 * last)
-    answer(2 * last + 1)
+    for t in (2, 3):
+        answer(2 * plane_at(t))
+        answer(2 * plane_at(t) + 1)
 
     for f in range(F):
         full = states[f]
@@ -327,18 +381,21 @@
         split[f, 0:K, :] = head
         split[f, K : 2 * K, :] = (full - head.astype(F32)).astype(jnp.bfloat16)
 
-    whole(gp.at[pl.ds(0, 15)], plane_recv.at[0]).wait()
-    total = gp[0]
-    for i in range(1, 16):
-        total = total + gp[i]
-    gy[y] = total
-    adding = [
-        copy_to(gy.at[y], gy.at[y], 3 + step, {"cells": ys[step] * 16 + here, "members": core})
-        for step in (2, 1, 3)
-    ]
-    for made in adding:
-        made.wait_recv()
-    gc[core] = (gy[0] + gy[1]) + (gy[2] + gy[3])
+    whole(g1.at[pl.ds(0, 7)], plane_recv.at[0]).wait()
+
+    def summed(ref):
+        return ((ref[0] + ref[1]) + (ref[2] + ref[3])) + ((ref[4] + ref[5]) + (ref[6] + ref[7]))
+
+    second_at = y // 2 * 4 + z
+    g2[second_at] = summed(g1)
+    for across, dz in ((1, 2), (0, 2), (1, 1), (1, 3), (0, 1), (0, 3), (1, 0)):
+        target = (3 - y if across else y) * 16 + zs[dz] * 4 + x
+        pltpu.make_async_remote_copy(
+            src_ref=g2.at[second_at], dst_ref=g2.at[second_at], send_sem=plane_send.at[1],
+            recv_sem=plane_recv.at[1], device_id={"cells": target, "members": core},
+        ).start()
+    whole(g2.at[pl.ds(0, 7)], plane_recv.at[1]).wait()
+    gc[core] = summed(g2)
     adding = copy_to(gc.at[core], gc.at[core], 3, pair_id)
 
     whole(n3, back_recv.at[0]).wait()
@@ -361,10 +418,15 @@
     adding.wait_recv()
     total = gc[0] + gc[1]
 
+    turned = jnp.transpose(total)
     a = []
     for h in range(8):
-        packed = total[8 * (h % 4) : 8 * (h % 4) + 8]
-        packed = packed if h < 4 else pltpu.roll(packed, 64, 1)
+        if h < 4:
+            packed = total[8 * h : 8 * h + 8]
+        else:
+            left = jnp.concatenate([turned[8 * h : 8 * h + 8], jnp.zeros((8, 96), F32)], axis=1)
+            right = pltpu.roll(total[8 * h - 32 : 8 * h - 24], 64, 1)
+            packed = jnp.where(lane < 32, left, right)
         packed = jnp.where(lane == sub + 8 * h, packed + (K - 1.0), packed)
         a.append(jnp.where(lane < K, packed, 0.0))
     inv = []
@@ -420,7 +482,7 @@
         for i in range(8):
             final = jnp.where(sub == i, rows[i] * jnp.sqrt(over[i]), final)
         inv.append(jnp.where(lane <= sub + first, final, 0.0))
-    cross_row = jnp.where(lane[0:1] < K, total[32:33, :], 0.0)
+    cross_row = jnp.concatenate([turned[64:65], turned[65:66], jnp.zeros((1, 64), F32)], axis=1)
     columns = jnp.zeros((8, 128), F32)
     weights = jnp.zeros((8, 128), F32)
     means = []
@@ -442,24 +504,31 @@
     head = own.astype(jnp.bfloat16)
     tail = (own - head.astype(F32)).astype(jnp.bfloat16)
     both = jnp.concatenate([head, tail], axis=0)
-    stores = []
     for f in range(F):
         product = jnp.dot(both, split[f], preferred_element_type=F32)
         out[f] = product[0:KL] + product[KL : 2 * KL]
-        stores.append(pltpu.make_async_copy(out.at[f], out_hbm.at[:, f], bulk.at[f]))
-        stores[-1].start()
 
     joined.wait_recv()
     for t in range(2):
         innov_out[:, 128 * t : 128 * t + 128] = part[0, t] + part[1, t]
     for made in sent:
-        made.wait_send()
+        if made is not swap:
+            made.wait_send()
     for ref, sem in (
-        (m3.at[pl.ds(0, 63)], ask_send), (n3.at[pl.ds(0, 63)], back_send), (gp.at[pl.ds(0, 15)], plane_send),
+        (m3.at[pl.ds(0, 63)], ask_send), (n3.at[pl.ds(0, 63)], back_send), (halo_in, halo_send),
     ):
         whole(ref, sem.at[0]).wait()
-    for made in stores:
-        made.wait()
+    whole(g1.at[pl.ds(0, 7)], plane_send.at[0]).wait()
+    whole(g2.at[pl.ds(0, 7)], plane_send.at[1]).wait()
+
+
+def write_out(by_field, innovation, out_hbm, innov_hbm, sems):
+    made = [pltpu.make_async_copy(innovation, innov_hbm, sems.at[F])]
+    made += [pltpu.make_async_copy(by_field.at[f], out_hbm.at[:, f], sems.at[f]) for f in range(F)]
+    for copy in made:
+        copy.start()
+    for copy in made:
+        copy.wait()
 
 
 def shards(
@@ -471,14 +540,13 @@
     analysis, innovation = pl.pallas_call(
         kernel,
         out_shape=(
-            jax.ShapeDtypeStruct((KL, F, CELLS), F32),
-            jax.ShapeDtypeStruct((1, 256), F32),
+            pltpu.VMEM((F, KL, CELLS), F32),
+            pltpu.VMEM((1, 256), F32),
         ),
         in_specs=[hbm] * 9,
-        out_specs=(hbm, vmem),
+        out_specs=(vmem, vmem),
         scratch_shapes=[
             pltpu.VMEM((F * KL, CELLS), F32),
-            pltpu.VMEM((F, KL, CELLS), F32),
             pltpu.VMEM((1, CELLS), F32),
             pltpu.VMEM((1, CELLS), I32),
             pltpu.SMEM((F, F), F32),
@@ -491,20 +559,24 @@
             pltpu.VMEM((F, 2 * K, CELLS), jnp.bfloat16),
             pltpu.VMEM((3, 8, CELLS), F32),
             pltpu.VMEM((2, 16, 128), F32),
-            pltpu.VMEM((2, 16, 128), F32),
-            pltpu.VMEM((128, 128), F32),
+            pltpu.VMEM((2, 2, 16, 128), F32),
+            pltpu.VMEM((2, 128, 128), F32),
+            pltpu.VMEM((2, 128, 128), F32),
+            pltpu.VMEM((2, 8, 128), F32),
+            pltpu.VMEM((8, 128), F32),
+            pltpu.VMEM((2, K, 256), F32),
             pltpu.VMEM((32, 1, 128), F32),
             pltpu.VMEM((64, 1, 128), F32),
             pltpu.VMEM((64, 128), I32),
             pltpu.VMEM((64, 128), I32),
-            pltpu.VMEM((K, CELLS), F32),
-            pltpu.VMEM((8, CELLS), F32),
+            pltpu.VMEM((K, K), F32),
+            pltpu.VMEM((K, 128), F32),
             pltpu.VMEM((8, 1, 128), F32),
             pltpu.VMEM((64, 1, 128), F32),
             pltpu.VMEM((2, 2, 1, 128), F32),
-            pltpu.VMEM((16, 40, 128), F32),
-            pltpu.VMEM((4, 40, 128), F32),
-            pltpu.VMEM((2, 40, 128), F32),
+            pltpu.VMEM((8, 32, 128), F32),
+            pltpu.VMEM((8, 32, 128), F32),
+            pltpu.VMEM((2, 32, 128), F32),
             pltpu.VMEM((K, 128), F32),
             pltpu.SemaphoreType.DMA((8,)),
             pltpu.SemaphoreType.DMA((8,)),
@@ -513,6 +585,8 @@
             pltpu.SemaphoreType.DMA((8,)),
             pltpu.SemaphoreType.DMA((1,)),
             pltpu.SemaphoreType.DMA((1,)),
+            pltpu.SemaphoreType.DMA((2,)),
+            pltpu.SemaphoreType.DMA((2,)),
             pltpu.SemaphoreType.DMA((1,)),
             pltpu.SemaphoreType.DMA((1,)),
         ],
@@ -521,6 +595,16 @@
         ensemble, row(speed), row(direction), couple, row(obs_place), row(obs_field),
         row(obs_value), row(obs_sigma), send_count,
     )
+    analysis, innovation = pl.pallas_call(
+        write_out,
+        out_shape=(
+            jax.ShapeDtypeStruct((KL, F, CELLS), F32),
+            jax.ShapeDtypeStruct((1, 256), F32),
+        ),
+        in_specs=[vmem, vmem],
+        out_specs=(hbm, hbm),
+        scratch_shapes=[pltpu.SemaphoreType.DMA((F + 1,))],
+    )(*(pltpu.with_memory_space_constraint(a, pltpu.VMEM) for a in (analysis, innovation)))
     return analysis, innovation.reshape(256)
 
 

time: 38.8 us -> 34.1 us (0.88)
  local copies, waits for them, and re-layouts: 2.44 us -> 0 us
  Pallas kernels: 35.6 us -> 33.3 us
    unnamed x4 -> x0, local copies, waits for them, and re-layouts: 2.44 us -> none
    pallas_call x1 -> x2, Pallas kernels: 35.6 us -> 33.3 us  [the longest x1 32.5 us: shards(): pl.pallas_call(kernel, out_shape=(pltpu.VMEM((F, KL, CELLS), F32), pltpu....]
where the time goes in v4:
time: 34.1 us; the launch traced here: 34 us
  Pallas kernels  33.3 us (98%)
  between operations  0.64 us (2%)
    pallas_call x1, Pallas kernels, shards(): pl.pallas_call(kernel, out_shape=(pltpu.VMEM((F, KL, CELLS), F32), pltpu....  32.5 us
    pallas_call x1, Pallas kernels, shards(): pl.pallas_call(write_out, out_shape=(jax.ShapeDtypeStruct((KL, F, CELLS),...  0.83 us

profile of v4, /device:TPU:1, one launch (start us, length us, event | category | flops | bytes accessed | tf_op | source)
XLA Modules:
  0.0 34.0 jit_solution(10844107669431664051)
XLA Ops:
  0.6 32.5 %shard_map.104 = (f32[4,32,1024]{2,1,0:T(8,128)S(1)}, f32[1,256]{1,0:T(1,128)S(1)}) custom-call(f32[32,4,1024]{2,1,0:T(4,128)} %ens_hbm.1, f32[1,1024]{1,0:T(1,128)} %bitcast.7, s32[1,1024]{1,0:T(1,128)} %bitcast.8, f32[4,4]{1,0:T(4,128)} %couple_hbm.1, s32[1,256]{1,0:T(1,128)} %bitcast.9, s32[1,256]{1,0:T(1,128)} %bitcast.10, f32[1,256]{1,0:T(1,128)} %bitcast.11, ...), custom_call_target="tpu_custom_call" | custom-call | tf_op jit(solution)/shard_map/pallas_call | solution.py:540
  33.2 0.8 %shard_map.105 = (f32[32,4,1024]{2,1,0:T(4,128)}, f32[1,256]{1,0:T(1,128)}) custom-call(f32[4,32,1024]{2,1,0:T(8,128)S(1)} %get-tuple-element.6.by_field, f32[1,256]{1,0:T(1,128)S(1)} %get-tuple-element.7.innovation), custom_call_target="tpu_custom_call" | custom-call | tf_op jit(solution)/shard_map/pallas_call | solution.py:598

commit v5 on v4

--- a/solution.py
+++ b/solution.py
@@ -15,8 +15,6 @@
 CELLS = 1024
 FAR = (2, 1, 3, 0)
 PLANE = [(dx, dz) for dx in FAR for dz in FAR]
-AWAY = [(dx, dz, dy) for dy in FAR for dx, dz in PLANE if dx or dz or dy]
-HALF = 16
 F32 = jnp.float32
 I32 = jnp.int32
 HIGHEST = lax.Precision.HIGHEST
@@ -32,7 +30,7 @@
     ens, speed, direction, couple, place, field, value, sigma, counts,
     states, split, coef, halo_out, halo_in, edge, base, keep, places, raw,
     m0, m3, starts_s, counts_s, gram_s, cross_s,
-    n0, n3, part, g1, g2, gc, mix, send, recv, bulk,
+    n0, n3, part, g1, g2, gc, e1, e2, ec, mix, send, recv, bulk,
     ask_send, ask_recv, back_send, back_recv, plane_send, plane_recv, halo_send, halo_recv,
 ):
     cells = lax.axis_index("cells")
@@ -46,18 +44,57 @@
     xs = [lax.rem(x + d, 4) for d in range(4)]
     zs = [lax.rem(z + d, 4) for d in range(4)]
     ys = [lax.rem(y + d, 4) for d in range(4)]
-    half_row = [t // 2 for t in ys]
+    parity = lax.rem(x, 2)
     in_plane = {(dx, dz): zs[dz] * 4 + xs[dx] for dx, dz in PLANE}
-    asked_row = {(dx, dz): xs[dx] * 8 + zs[dz] * 2 for dx, dz in PLANE}
+    own_ys = [lax.rem(y + core + 2 * i, 4) for i in range(2)]
+    served_x = [lax.rem(x + lax.rem(x + core, 2) + 2 * i, 4) for i in range(2)]
+    alone = core + parity == 0
+    early_at = x + core * (z - x)
+    late_at = z + core * (x - z)
+    early_stride = 1 + 3 * core
+    late_stride = 4 - 3 * core
+    beside = y + 1 - 2 * lax.rem(y, 2)
+    group1, group2 = [], []
+    for across, step in ((1, 2), (0, 2), (1, 1), (1, 3), (0, 1), (0, 3), (1, 0)):
+        along = lax.rem(early_at + step, 4) * early_stride + late_at * late_stride
+        group1.append({"cells": (beside if across else y) * 16 + along, "members": core})
+        along = lax.rem(late_at + step, 4) * late_stride + early_at * early_stride
+        group2.append({"cells": (3 - y if across else y) * 16 + along, "members": core})
+    asked_of = [
+        (own_ys[i] * 16 + in_plane[dx, dz], i * 16 + in_plane[dx, dz], (dx, dz, i))
+        for i in (1, 0) for dx, dz in PLANE
+    ]
 
     barrier = pltpu.get_barrier_semaphore()
 
-    for dx, dz, dy in AWAY:
-        target = ys[dy] * 16 + in_plane[dx, dz]
-        pl.semaphore_signal(barrier, inc=1, device_id={"cells": target, "members": core})
+    for target, _, at in asked_of[:-1]:
+        pl.semaphore_signal(barrier, inc=1, device_id={"cells": target, "members": parity})
+    for dy in (2, 1, 3, 0):
+        for dz in FAR:
+            for i in (1, 0):
+                if (dy, dz, i) != (0, 0, 0):
+                    target = ys[dy] * 16 + zs[dz] * 4 + served_x[i]
+                    pl.semaphore_signal(
+                        barrier, inc=1, device_id={"cells": target, "members": dy % 2}
+                    )
+    for device in group1 + group2:
+        pl.semaphore_signal(barrier, inc=1, device_id=device)
+    @pl.when(jnp.logical_not(alone))
+    def _():
+        pl.semaphore_signal(
+            barrier, inc=1, device_id={"cells": asked_of[-1][0], "members": parity}
+        )
+
+    @pl.when(jnp.logical_not(alone))
+    def _():
+        pl.semaphore_signal(
+            barrier, inc=1, device_id={"cells": y * 16 + z * 4 + served_x[0], "members": 0}
+        )
+
     pl.semaphore_signal(barrier, inc=1, device_id=pair_id)
     for neighbour in (left_id, right_id):
-        pl.semaphore_signal(barrier, inc=1, device_id={"cells": neighbour, "members": 1 - core})
+        for to in range(2):
+            pl.semaphore_signal(barrier, inc=1, device_id={"cells": neighbour, "members": to})
     small = (
         (counts_hbm, counts), (place_hbm, place), (field_hbm, field), (value_hbm, value),
         (sigma_hbm, sigma), (speed_hbm, speed), (direction_hbm, direction), (couple_hbm, couple),
@@ -105,31 +142,25 @@
         number = jnp.sum(jnp.where(lane64 == owner, count_row, 0), axis=1, keepdims=True)
         return begin, number
 
-    slot = lane % 16
-    which = (lane // 16) % 4
-    upper = lane >= 64
+    slot = lane % 32
+    which = lane // 32
     for g in range(4):
         row = sub64 + 8 * g
-        lower = (row // 2) % 4 * 4 + row // 8 + (row % 2) * 32
-        b0, c0 = start_and_count(lower)
-        b1, c1 = start_and_count(lower + 16)
-        begin = jnp.where(upper, b1, b0)
-        number = jnp.where(upper, c1, c0)
-        rank = slot + HALF * core
-        position = begin + rank
+        owner_y = own_ys[g // 2]
+        begin, number = start_and_count(owner_y * 16 + row % 16)
+        begin = jnp.broadcast_to(begin, (8, 128))
+        number = jnp.broadcast_to(number, (8, 128))
+        starts_s[8 * g : 8 * g + 8, :] = begin
+        counts_s[8 * g : 8 * g + 8, :] = number
+        position = begin + slot
         low = position & 127
         second = position >= 128
         found = jnp.zeros((8, 128), F32)
         for q in range(3):
             got = jnp.where(second, lanes_of(tables[q][1], low), lanes_of(tables[q][0], low))
             found = jnp.where(which == q, got, found)
-        found = jnp.where(rank < number, found, 0.0)
+        found = jnp.where(slot < number, found, 0.0)
         m0[8 * g : 8 * g + 8] = found.reshape(8, 1, 128)
-    for g in range(8):
-        row = sub64 + 8 * g
-        begin, number = start_and_count(row)
-        starts_s[8 * g : 8 * g + 8, :] = jnp.broadcast_to(begin, (8, 128))
-        counts_s[8 * g : 8 * g + 8, :] = jnp.broadcast_to(number, (8, 128))
 
     for made in loads:
         made.wait()
@@ -188,32 +219,56 @@
 
     lax.fori_loop(0, 2, interior, 0)
 
-    pl.semaphore_wait(barrier, 66)
-
-    for to in range(2):
-        for side, neighbour in ((0, right_id), (1, left_id)):
-            pltpu.make_async_remote_copy(
-                src_ref=halo_out.at[side], dst_ref=halo_in.at[side, core],
-                send_sem=halo_send.at[0], recv_sem=halo_recv.at[0],
-                device_id={"cells": neighbour, "members": to},
-            ).start()
+    pl.semaphore_wait(barrier, 83 - 2 * jnp.where(alone, 1, 0))
+
+    sides = ((0, right_id, cells < 63, cells > 0), (1, left_id, cells > 0, cells < 63))
+    for side, neighbour, sends, _ in sides:
+
+        @pl.when(sends)
+        def _():
+            for to in range(2):
+                pltpu.make_async_remote_copy(
+                    src_ref=halo_out.at[side], dst_ref=halo_in.at[side, core],
+                    send_sem=halo_send.at[side], recv_sem=halo_recv.at[side],
+                    device_id={"cells": neighbour, "members": to},
+                ).start()
+
+        @pl.when(jnp.logical_not(sends))
+        def _():
+            halo_in[1 - side] = jnp.zeros((2, 16, 128), F32)
+
     based = copy_to(base.at[core], base.at[core], 0, pair_id)
-    for dx, dz, dy in AWAY:
-        target = ys[dy] * 16 + in_plane[dx, dz]
+    source_at = y * 8 + z * 2 + x // 2
+
+    def ask(target, row):
         pltpu.make_async_remote_copy(
-            src_ref=m0.at[asked_row[dx, dz] + half_row[dy]], dst_ref=m3.at[cells],
-            send_sem=ask_send.at[0], recv_sem=ask_recv.at[cells // 8],
-            device_id={"cells": target, "members": core},
+            src_ref=m0.at[row], dst_ref=m3.at[source_at], send_sem=ask_send.at[0],
+            recv_sem=ask_recv.at[cells // 8], device_id={"cells": target, "members": parity},
         ).start()
-    own_row = asked_row[0, 0] + half_row[0]
-    pltpu.make_async_copy(m0.at[own_row], m3.at[cells], ask_recv.at[cells // 8]).start()
+
+    for target, row, at in asked_of[:-1]:
+        ask(target, row)
+
+    @pl.when(jnp.logical_not(alone))
+    def _():
+        ask(*asked_of[-1][:2])
+
+    @pl.when(alone)
+    def _():
+        pltpu.make_async_copy(m0.at[asked_of[-1][1]], m3.at[source_at], ask_recv.at[cells // 8]).start()
+
     lax.fori_loop(2, 4, interior, 0)
 
     mine = states.at[:, pl.ds(pl.multiple_of(core * KL, KL), KL), :]
     swap = copy_to(mine, mine, 2, pair_id)
 
     based.wait_recv()
-    whole(halo_in, halo_recv.at[0]).wait()
+    for side, _, _, receives in sides:
+
+        @pl.when(receives)
+        def _():
+            whole(halo_in.at[side], halo_recv.at[side]).wait()
+
     swap.wait()
     has_left = jnp.where(cells > 0, 1.0, 0.0).astype(F32)
     has_right = jnp.where(cells < 63, 1.0, 0.0).astype(F32)
@@ -254,24 +309,28 @@
                 states[f, into, CELLS - 128 :] = jnp.where(lane >= 124, pltpu.roll(made, 64, 1), last)
         return carry
 
-    lax.fori_loop(0, 2, border, 0)
-
-    off = lax.rem(y, 2) * 64
+    for m in range(2):
+        border(m, 0)
+
 
     def answer(r):
-        for i in range(8):
-            source = 8 * r + i
-
-            @pl.when(source != cells)
+        back_y = lax.rem(y + 4 - r // 2, 4)
+        back_row = back_y // 2 * 16 + z * 4 + x
+        for i in range(4):
+            source = r * 8 + i // 2 * 4 + i % 2 * 2 + core
+            itself = jnp.logical_and(source == cells, core == 0)
+
+            @pl.when(jnp.logical_not(itself))
             def _():
                 pltpu.make_async_remote_copy(
-                    src_ref=n0.at[r], dst_ref=n3.at[cells], send_sem=back_send.at[0],
-                    recv_sem=back_recv.at[0], device_id={"cells": source, "members": core},
+                    src_ref=n0.at[r], dst_ref=n3.at[back_row], send_sem=back_send.at[0],
+                    recv_sem=back_recv.at[0],
+                    device_id={"cells": source, "members": lax.rem(back_y, 2)},
                 ).start()
 
-            @pl.when(source == cells)
+            @pl.when(itself)
             def _():
-                pltpu.make_async_copy(n0.at[r], n3.at[cells], back_recv.at[0]).start()
+                pltpu.make_async_copy(n0.at[r], n3.at[back_row], back_recv.at[0]).start()
 
     def plane_at(t):
         step = t + t // 2 - 2 * (t // 3)
@@ -305,15 +364,16 @@
     def arrived(plane):
         for pair in range(2):
             r = 2 * plane + pair
-            whole(m3.at[pl.ds(8 * r, 8)], ask_recv.at[r]).wait()
+            whole(m3.at[pl.ds(4 * r, 4)], ask_recv.at[r]).wait()
 
     def prepare(plane, turn):
         for pair in range(2):
-            rows = m3[pl.ds(8 * (2 * plane + pair), 8)].reshape(8, 128)
+            rows = m3[pl.ds(4 * (2 * plane + pair), 4)].reshape(4, 128)
+            rows = jnp.concatenate([rows, rows], axis=0)
             asked = []
             for q in range(3):
-                got = lanes_of(rows, off + 16 * q + slot)
-                got = jnp.where(lane // 16 == sub, got, 0.0)
+                got = lanes_of(rows, 32 * q + slot)
+                got = jnp.where(which == sub, got, 0.0)
                 asked.append(jnp.sum(got, axis=0, keepdims=True))
             places[pair : pair + 1, :] = asked[0]
             keep[turn, pair : pair + 1, :] = asked[1]
@@ -354,23 +414,24 @@
     lax.fori_loop(0, 4, pick, 0)
     finish(plane_at(3), 1)
 
-    cross = jnp.sum(cross_s[...], axis=1, keepdims=True)
     gram = gram_s[...]
-    apart = lax.broadcasted_iota(I32, (32, 64), 1)
-    lower = jnp.where(
-        apart >= 32, gram[32:64],
-        jnp.where(apart == 0, cross[0:32], jnp.where(apart == 1, cross[32:64], 0.0)),
-    )
-    first_at = lax.rem(y, 2) * 4 + x
-    g1[first_at] = jnp.concatenate([gram[0:32], lower], axis=1)
-
-    beside = y + 1 - 2 * lax.rem(y, 2)
-    for across, dx in ((1, 2), (0, 2), (1, 1), (1, 3), (0, 1), (0, 3), (1, 0)):
-        target = (beside if across else y) * 16 + z * 4 + xs[dx]
-        pltpu.make_async_remote_copy(
-            src_ref=g1.at[first_at], dst_ref=g1.at[first_at], send_sem=plane_send.at[0],
-            recv_sem=plane_recv.at[0], device_id={"cells": target, "members": core},
-        ).start()
+    row32 = lax.broadcasted_iota(I32, (32, 32), 0)
+    col32 = lax.broadcasted_iota(I32, (32, 32), 1)
+    last_block = gram[32:64, 32:64]
+    triangles = jnp.where(col32 >= row32, gram[0:32, 0:32], last_block)
+    diagonal = jnp.sum(jnp.where(col32 == row32, last_block, 0.0), axis=0, keepdims=True)
+    crosses = jnp.sum(jnp.transpose(cross_s[...]), axis=0, keepdims=True)
+    blocks = jnp.concatenate([triangles, gram[0:32, 32:64]], axis=1)
+    first_at = lax.rem(y, 2) * 4 + early_at
+    g1[first_at] = jnp.concatenate([blocks[0:16], blocks[16:32]], axis=1)
+    e1[first_at] = jnp.concatenate([diagonal, crosses, jnp.zeros((1, 32), F32)], axis=1)
+
+    for device in group1:
+        for i, ref in enumerate((g1, e1)):
+            pltpu.make_async_remote_copy(
+                src_ref=ref.at[first_at], dst_ref=ref.at[first_at], send_sem=plane_send.at[i],
+                recv_sem=plane_recv.at[i], device_id=device,
+            ).start()
     for t in (2, 3):
         answer(2 * plane_at(t))
         answer(2 * plane_at(t) + 1)
@@ -382,33 +443,37 @@
         split[f, K : 2 * K, :] = (full - head.astype(F32)).astype(jnp.bfloat16)
 
     whole(g1.at[pl.ds(0, 7)], plane_recv.at[0]).wait()
+    whole(e1.at[pl.ds(0, 7)], plane_recv.at[1]).wait()
 
     def summed(ref):
         return ((ref[0] + ref[1]) + (ref[2] + ref[3])) + ((ref[4] + ref[5]) + (ref[6] + ref[7]))
 
-    second_at = y // 2 * 4 + z
+    second_at = y // 2 * 4 + late_at
     g2[second_at] = summed(g1)
-    for across, dz in ((1, 2), (0, 2), (1, 1), (1, 3), (0, 1), (0, 3), (1, 0)):
-        target = (3 - y if across else y) * 16 + zs[dz] * 4 + x
-        pltpu.make_async_remote_copy(
-            src_ref=g2.at[second_at], dst_ref=g2.at[second_at], send_sem=plane_send.at[1],
-            recv_sem=plane_recv.at[1], device_id={"cells": target, "members": core},
-        ).start()
-    whole(g2.at[pl.ds(0, 7)], plane_recv.at[1]).wait()
+    e2[second_at] = summed(e1)
+    for device in group2:
+        for i, ref in enumerate((g2, e2)):
+            pltpu.make_async_remote_copy(
+                src_ref=ref.at[second_at], dst_ref=ref.at[second_at], send_sem=plane_send.at[2 + i],
+                recv_sem=plane_recv.at[2 + i], device_id=device,
+            ).start()
+    whole(g2.at[pl.ds(0, 7)], plane_recv.at[2]).wait()
+    whole(e2.at[pl.ds(0, 7)], plane_recv.at[3]).wait()
     gc[core] = summed(g2)
+    ec[core] = summed(e2)
+    adding_row = copy_to(ec.at[core], ec.at[core], 4, pair_id)
     adding = copy_to(gc.at[core], gc.at[core], 3, pair_id)
 
     whole(n3, back_recv.at[0]).wait()
-    shift = 16 * lax.rem(cells, 8) - HALF * core
+    shift = 64 * lax.rem(z, 2) + 32 * (x // 2)
     totals = [jnp.zeros((8, 128), F32)] * 2
-    for g in range(8):
+    for g in range(4):
         rows = n3[8 * g : 8 * g + 8].reshape(8, 128)
         begin = starts_s[8 * g : 8 * g + 8, :]
         number = counts_s[8 * g : 8 * g + 8, :]
         for t in range(2):
             rank = lane + 128 * t - begin
-            inside = rank - HALF * core
-            good = (inside >= 0) & (inside < HALF) & (rank < number)
+            good = (rank >= 0) & (rank < number)
             got = lanes_of(rows, (rank + shift) & 127)
             totals[t] = totals[t] + jnp.where(good, got, 0.0)
     for t in range(2):
@@ -416,17 +481,24 @@
     joined = copy_to(part.at[core], part.at[core], 7, pair_id)
 
     adding.wait_recv()
+    adding_row.wait_recv()
     total = gc[0] + gc[1]
-
-    turned = jnp.transpose(total)
+    extra = ec[0] + ec[1]
+
+    upright = jnp.concatenate([total, pltpu.roll(total, 64, 1)], axis=0)
+    turned = jnp.transpose(upright)
+    diagonals = jnp.broadcast_to(extra, (8, 128))
     a = []
     for h in range(8):
+        at = 8 * h % 32
+        own_rows = upright[at : at + 8]
+        flipped = jnp.concatenate([turned[at : at + 8], jnp.zeros((8, 96), F32)], axis=1)
         if h < 4:
-            packed = total[8 * h : 8 * h + 8]
+            packed = jnp.where(lane >= 32, own_rows, jnp.where(lane >= sub + at, own_rows, flipped))
         else:
+            corner = jnp.where(lane < sub + at, own_rows, jnp.where(lane == sub + at, diagonals, flipped))
             left = jnp.concatenate([turned[8 * h : 8 * h + 8], jnp.zeros((8, 96), F32)], axis=1)
-            right = pltpu.roll(total[8 * h - 32 : 8 * h - 24], 64, 1)
-            packed = jnp.where(lane < 32, left, right)
+            packed = jnp.where(lane < 32, left, pltpu.roll(corner, 32, 1))
         packed = jnp.where(lane == sub + 8 * h, packed + (K - 1.0), packed)
         a.append(jnp.where(lane < K, packed, 0.0))
     inv = []
@@ -482,7 +554,7 @@
         for i in range(8):
             final = jnp.where(sub == i, rows[i] * jnp.sqrt(over[i]), final)
         inv.append(jnp.where(lane <= sub + first, final, 0.0))
-    cross_row = jnp.concatenate([turned[64:65], turned[65:66], jnp.zeros((1, 64), F32)], axis=1)
+    cross_row = jnp.where(lane[0:1] < K, pltpu.roll(diagonals, 96, 1)[0:1], 0.0)
     columns = jnp.zeros((8, 128), F32)
     weights = jnp.zeros((8, 128), F32)
     means = []
@@ -515,11 +587,23 @@
         if made is not swap:
             made.wait_send()
     for ref, sem in (
-        (m3.at[pl.ds(0, 63)], ask_send), (n3.at[pl.ds(0, 63)], back_send), (halo_in, halo_send),
+        (m3.at[pl.ds(0, 31)], ask_send), (n3.at[pl.ds(0, 31)], back_send),
     ):
         whole(ref, sem.at[0]).wait()
-    whole(g1.at[pl.ds(0, 7)], plane_send.at[0]).wait()
-    whole(g2.at[pl.ds(0, 7)], plane_send.at[1]).wait()
+
+    @pl.when(jnp.logical_not(alone))
+    def _():
+        whole(m3.at[0], ask_send.at[0]).wait()
+        whole(n3.at[0], back_send.at[0]).wait()
+
+    for side, _, sends, _ in sides:
+
+        @pl.when(sends)
+        def _():
+            whole(halo_in.at[side], halo_send.at[side]).wait()
+
+    for i, ref in enumerate((g1, e1, g2, e2)):
+        whole(ref.at[pl.ds(0, 7)], plane_send.at[i]).wait()
 
 
 def write_out(by_field, innovation, out_hbm, innov_hbm, sems):
@@ -566,17 +650,20 @@
             pltpu.VMEM((8, 128), F32),
             pltpu.VMEM((2, K, 256), F32),
             pltpu.VMEM((32, 1, 128), F32),
-            pltpu.VMEM((64, 1, 128), F32),
-            pltpu.VMEM((64, 128), I32),
-            pltpu.VMEM((64, 128), I32),
+            pltpu.VMEM((32, 1, 128), F32),
+            pltpu.VMEM((32, 128), I32),
+            pltpu.VMEM((32, 128), I32),
             pltpu.VMEM((K, K), F32),
             pltpu.VMEM((K, 128), F32),
             pltpu.VMEM((8, 1, 128), F32),
-            pltpu.VMEM((64, 1, 128), F32),
+            pltpu.VMEM((32, 1, 128), F32),
             pltpu.VMEM((2, 2, 1, 128), F32),
-            pltpu.VMEM((8, 32, 128), F32),
-            pltpu.VMEM((8, 32, 128), F32),
-            pltpu.VMEM((2, 32, 128), F32),
+            pltpu.VMEM((8, 16, 128), F32),
+            pltpu.VMEM((8, 16, 128), F32),
+            pltpu.VMEM((2, 16, 128), F32),
+            pltpu.VMEM((8, 1, 128), F32),
+            pltpu.VMEM((8, 1, 128), F32),
+            pltpu.VMEM((2, 1, 128), F32),
             pltpu.VMEM((K, 128), F32),
             pltpu.SemaphoreType.DMA((8,)),
             pltpu.SemaphoreType.DMA((8,)),
@@ -585,10 +672,10 @@
             pltpu.SemaphoreType.DMA((8,)),
             pltpu.SemaphoreType.DMA((1,)),
             pltpu.SemaphoreType.DMA((1,)),
+            pltpu.SemaphoreType.DMA((4,)),
+            pltpu.SemaphoreType.DMA((4,)),
             pltpu.SemaphoreType.DMA((2,)),
             pltpu.SemaphoreType.DMA((2,)),
-            pltpu.SemaphoreType.DMA((1,)),
-            pltpu.SemaphoreType.DMA((1,)),
         ],
         compiler_params=pltpu.CompilerParams(collective_id=0, has_side_effects=True),
     )(

time: 34.1 us -> 33.1 us (0.971)
  Pallas kernels: 33.3 us -> 32.3 us
    pallas_call x1, Pallas kernels: 32.5 us -> 31.5 us  [shards(): pl.pallas_call(kernel, out_shape=(pltpu.VMEM((F, KL, CELLS), F32), pltpu....]
where the time goes in v5:
time: 33.1 us; the launch traced here: 33 us
  Pallas kernels  32.3 us (98%)
  between operations  0.64 us (2%)
    pallas_call x1, Pallas kernels, shards(): pl.pallas_call(kernel, out_shape=(pltpu.VMEM((F, KL, CELLS), F32), pltpu....  31.5 us
    pallas_call x1, Pallas kernels, shards(): pl.pallas_call(write_out, out_shape=(jax.ShapeDtypeStruct((KL, F, CELLS),...  0.83 us

profile of v5, /device:TPU:1, one launch (start us, length us, event | category | flops | bytes accessed | tf_op | source)
XLA Modules:
  0.0 33.0 jit_solution(13999588708066872089)
XLA Ops:
  0.6 31.5 %shard_map.104 = (f32[4,32,1024]{2,1,0:T(8,128)S(1)}, f32[1,256]{1,0:T(1,128)S(1)}) custom-call(f32[32,4,1024]{2,1,0:T(4,128)} %ens_hbm.1, f32[1,1024]{1,0:T(1,128)} %bitcast.7, s32[1,1024]{1,0:T(1,128)} %bitcast.8, f32[4,4]{1,0:T(4,128)} %couple_hbm.1, s32[1,256]{1,0:T(1,128)} %bitcast.9, s32[1,256]{1,0:T(1,128)} %bitcast.10, f32[1,256]{1,0:T(1,128)} %bitcast.11, ...), custom_call_target="tpu_custom_call" | custom-call | tf_op jit(solution)/shard_map/pallas_call | solution.py:624
  32.1 0.8 %shard_map.105 = (f32[32,4,1024]{2,1,0:T(4,128)}, f32[1,256]{1,0:T(1,128)}) custom-call(f32[4,32,1024]{2,1,0:T(8,128)S(1)} %get-tuple-element.6.by_field, f32[1,256]{1,0:T(1,128)S(1)} %get-tuple-element.7.innovation), custom_call_target="tpu_custom_call" | custom-call | tf_op jit(solution)/shard_map/pallas_call | solution.py:685

commit v6 on v5

--- a/solution.py
+++ b/solution.py
@@ -217,7 +217,7 @@
             states[f, into, :] = made
         return carry
 
-    lax.fori_loop(0, 2, interior, 0)
+    lax.fori_loop(0, 1, interior, 0)
 
     pl.semaphore_wait(barrier, 83 - 2 * jnp.where(alone, 1, 0))
 
@@ -257,7 +257,7 @@
     def _():
         pltpu.make_async_copy(m0.at[asked_of[-1][1]], m3.at[source_at], ask_recv.at[cells // 8]).start()
 
-    lax.fori_loop(2, 4, interior, 0)
+    lax.fori_loop(1, 4, interior, 0)
 
     mine = states.at[:, pl.ds(pl.multiple_of(core * KL, KL), KL), :]
     swap = copy_to(mine, mine, 2, pair_id)

time: 33.1 us -> 33.1 us (level)
  no operation moved by 1% of the time
where the time goes in v6:
time: 33.1 us; the launch traced here: 33 us
  Pallas kernels  32.3 us (98%)
  between operations  0.64 us (2%)
    pallas_call x1, Pallas kernels, shards(): pl.pallas_call(kernel, out_shape=(pltpu.VMEM((F, KL, CELLS), F32), pltpu....  31.5 us
    pallas_call x1, Pallas kernels, shards(): pl.pallas_call(write_out, out_shape=(jax.ShapeDtypeStruct((KL, F, CELLS),...  0.83 us

profile of v6, /device:TPU:1, one launch (start us, length us, event | category | flops | bytes accessed | tf_op | source)
XLA Modules:
  0.0 33.0 jit_solution(19932305422275608)
XLA Ops:
  0.6 31.5 %shard_map.104 = (f32[4,32,1024]{2,1,0:T(8,128)S(1)}, f32[1,256]{1,0:T(1,128)S(1)}) custom-call(f32[32,4,1024]{2,1,0:T(4,128)} %ens_hbm.1, f32[1,1024]{1,0:T(1,128)} %bitcast.7, s32[1,1024]{1,0:T(1,128)} %bitcast.8, f32[4,4]{1,0:T(4,128)} %couple_hbm.1, s32[1,256]{1,0:T(1,128)} %bitcast.9, s32[1,256]{1,0:T(1,128)} %bitcast.10, f32[1,256]{1,0:T(1,128)} %bitcast.11, ...), custom_call_target="tpu_custom_call" | custom-call | tf_op jit(solution)/shard_map/pallas_call | solution.py:624
  32.1 0.8 %shard_map.105 = (f32[32,4,1024]{2,1,0:T(4,128)}, f32[1,256]{1,0:T(1,128)}) custom-call(f32[4,32,1024]{2,1,0:T(8,128)S(1)} %get-tuple-element.6.by_field, f32[1,256]{1,0:T(1,128)S(1)} %get-tuple-element.7.innovation), custom_call_target="tpu_custom_call" | custom-call | tf_op jit(solution)/shard_map/pallas_call | solution.py:685
